TPU v7x, 512 devices: a whole 4x4x16 slice. The times are simulated.
512 devices in a mesh: seq: 32 (over x, y, core), exp: 16 (over z).
Axes of the slice: x: 4, y: 4, z: 16, core: 2. Of those that a mesh axis runs over, the one named last changes fastest.
Arguments:
- hidden_in: bfloat16 [16, 4096, 2048], P('exp', 'seq'), may hold values from -6 to 6
- route_ids: int32 [16, 4096, 2], P('exp', 'seq'), may hold values from 0 to 15, all different within a row; in each aligned block of 128 rows (0 to 127, 128 to 255, ..., all dimensions but the last counted through in order) at most 32 rows name the same one
- route_gates: float32 [16, 4096, 2], P('exp', 'seq'), may hold values from 0.1 to 1
- language: int32 [16, 4096], P('exp', 'seq'), may hold values from 0 to 7
- allowed: int32 [8, 8], replicated, may hold values from 0 to 15, all different within a row
- w_gate: bfloat16 [16, 2048, 512], P('exp', 'seq'), may hold values from -0.125 to 0.125
- w_up: bfloat16 [16, 2048, 512], P('exp', 'seq'), may hold values from -0.125 to 0.125
- w_down: bfloat16 [16, 512, 2048], P('exp', 'seq'), may hold values from -0.25 to 0.25
- gate_proj: bfloat16 [2048, 64], replicated, may hold values from -0.125 to 0.125
- head_decay: float32 [32], replicated, may hold values from -13 to -2
- query_in: bfloat16 [16, 4096, 2048], P('exp', 'seq'), may hold values from -6 to 6
- key_in: bfloat16 [16, 4096, 2048], P('exp', 'seq'), may hold values from -6 to 6
- value_in: bfloat16 [16, 4096, 4096], P('exp', 'seq'), may hold values from -6 to 6
- block_inverse: bfloat16 [16, 4096, 2048], P('exp', 'seq'), may hold values from -0.29882812 to 0.29882812
Outputs:
- routed: bfloat16 [16, 4096, 2048], P('exp', 'seq')
- core_out: bfloat16 [16, 4096, 4096], P('exp', 'seq')
Inputs may be any that keep to these rules, and one draw needn't show every extreme that they name: `route_ids`: among the routes of the rows of one device, no expert is named more than 32 times, a bound that some block reaches. `allowed`: each of its rows names 8 different experts, and every expert is allowed for some language.
All inputs are finite; a program needn't handle non-finite values.
Results may differ from a plain program's by a relative error of at most 0.019.
Values may be sent and summed in bfloat16 or wider, within the bound.
A program may use at most 64 MiB of HBM per device.

v0:
```python
import jax
import jax.numpy as jnp
from jax import lax
from jax.sharding import PartitionSpec as P

highest = lax.Precision.HIGHEST


def normalized(values, head_count, factor_scale):
    flat_vals = values.astype(jnp.float32)
    shaped = flat_vals.reshape(flat_vals.shape[0], head_count, -1)
    factor = lax.rsqrt(jnp.sum(shaped * shaped, axis=-1, keepdims=True) + 1e-06) * factor_scale
    return (shaped * factor).astype(jnp.bfloat16)


def delta_blocks(queries, key_rows, values, inverse, beta_gate, decay_log):
    head_count, block_count, block_size, key_dim = queries.shape
    value_dim = values.shape[-1]
    cumulative = jnp.cumsum(decay_log, axis=-1)
    eye_mat = jnp.eye(block_size, dtype=jnp.float32)
    strict = jnp.tril(jnp.ones((block_size, block_size), jnp.float32), -1)
    causal = jnp.tril(jnp.ones((block_size, block_size), jnp.bool_))
    solver = (eye_mat + strict * inverse.astype(jnp.float32)).astype(jnp.bfloat16)
    beta_vals = (beta_gate[..., None] * values.astype(jnp.float32)).astype(jnp.bfloat16)
    beta_keys = (
        (beta_gate * jnp.exp(cumulative))[..., None] * key_rows.astype(jnp.float32)
    ).astype(jnp.bfloat16)
    new_base = jnp.einsum("hnij,hnjd->hnid", solver, beta_vals, preferred_element_type=jnp.float32)
    key_mix = jnp.einsum("hnij,hnjd->hnid", solver, beta_keys, preferred_element_type=jnp.float32)
    query_gate = queries.astype(jnp.float32) * jnp.exp(cumulative)[..., None]
    spread = jnp.where(causal, cumulative[..., :, None] - cumulative[..., None, :], 0.0)
    scores = jnp.einsum("hnid,hnjd->hnij", queries, key_rows, preferred_element_type=jnp.float32)
    weights = jnp.where(causal, scores * jnp.exp(spread), 0.0).astype(jnp.bfloat16)
    tail_decay = jnp.exp(cumulative[..., -1:] - cumulative)
    key_decay = (key_rows.astype(jnp.float32) * tail_decay[..., None]).astype(jnp.bfloat16)
    carry_decay = jnp.exp(cumulative[..., -1])

    def advance(carry_state, inputs):
        mix_now, base_now, gate_now, keyd_now, keep_now = inputs
        fresh_vals = (
            base_now - jnp.einsum("hid,hde->hie", mix_now, carry_state, precision=highest)
        ).astype(jnp.bfloat16)
        early_out = jnp.einsum("hid,hde->hie", gate_now, carry_state, precision=highest)
        carry_state = keep_now[:, None, None] * carry_state + jnp.einsum(
            "hid,hie->hde", keyd_now, fresh_vals, preferred_element_type=jnp.float32
        )
        return (carry_state, (fresh_vals, early_out))

    moved_seq = tuple(
        (
            jnp.moveaxis(element, 1, 0)
            for element in (key_mix, new_base, query_gate, key_decay, carry_decay)
        )
    )
    initial = jnp.zeros((head_count, key_dim, value_dim), jnp.float32)
    _, (fresh_vals, early_out) = lax.scan(advance, initial, moved_seq)
    fresh_vals = jnp.moveaxis(fresh_vals, 0, 1)
    early_out = jnp.moveaxis(early_out, 0, 1)
    local_out = jnp.einsum(
        "hnij,hnjd->hnid", weights, fresh_vals, preferred_element_type=jnp.float32
    )
    return (early_out + local_out).astype(jnp.bfloat16)


def per_device(
    hidden_in,
    route_ids,
    route_gates,
    language,
    allowed,
    w_gate,
    w_up,
    w_down,
    gate_proj,
    head_decay,
    query_in,
    key_in,
    value_in,
    block_inverse,
):
    exp_size = lax.axis_size("exp")
    seq_size = lax.axis_size("seq")
    tokens = hidden_in[0]
    tok_rows, model_width = tokens.shape
    routes_tok = route_ids.shape[2]
    experts = exp_size * w_gate.shape[0]
    capacity = 2 * tok_rows * routes_tok // experts
    flat_routes = route_ids[0].reshape(-1)
    expert_range = jnp.arange(experts, dtype=jnp.int32)
    onehot = (flat_routes[:, None] == expert_range[None, :]).astype(jnp.int32)
    earlier = jnp.cumsum(onehot, axis=0) - onehot
    slot_index = jnp.sum(earlier * onehot, axis=1)
    target = flat_routes * capacity + slot_index
    route_token = jnp.arange(tok_rows * routes_tok, dtype=jnp.int32) // routes_tok
    source_row = jnp.full((experts * capacity,), tok_rows, jnp.int32).at[target].set(route_token)
    padded = jnp.concatenate([tokens, jnp.zeros((1, model_width), tokens.dtype)], axis=0)
    outgoing = jnp.take(padded, source_row, axis=0).reshape(experts, capacity, model_width)
    incoming = lax.all_to_all(outgoing, "exp", split_axis=0, concat_axis=0, tiled=True)
    expert_rows = incoming.reshape(-1, model_width)

    def add_rows(portion):
        return jnp.dot(expert_rows, portion, preferred_element_type=jnp.float32)

    gate_proj_h = add_rows(lax.all_gather(w_gate[0], "seq", axis=0, tiled=True))
    up_proj_h = add_rows(lax.all_gather(w_up[0], "seq", axis=0, tiled=True))
    hidden = (jax.nn.silu(gate_proj_h) * up_proj_h).astype(jnp.bfloat16)
    produced = jnp.dot(
        hidden,
        lax.all_gather(w_down[0], "seq", axis=0, tiled=True),
        preferred_element_type=jnp.float32,
    )
    produced = produced.astype(jnp.bfloat16).reshape(exp_size, -1, model_width)
    returned = lax.all_to_all(produced, "exp", split_axis=0, concat_axis=0, tiled=True)
    back_rows = jnp.take(returned.reshape(-1, model_width), target, axis=0).reshape(
        tok_rows, routes_tok, model_width
    )
    lang_count = allowed.shape[0]
    lang_table = jnp.any(allowed[:, :, None] == expert_range[None, None, :], axis=1).astype(
        jnp.float32
    )
    lang_hot = (language[0][:, None] == jnp.arange(lang_count, dtype=jnp.int32)[None, :]).astype(
        jnp.float32
    )
    token_allow = jnp.dot(lang_hot, lang_table, precision=highest)
    route_allow = jnp.sum(
        token_allow[:, None, :] * onehot.reshape(tok_rows, routes_tok, experts).astype(jnp.float32),
        axis=2,
    )
    route_weight = route_gates[0] * route_allow
    mixed = jnp.sum(route_weight[..., None] * back_rows.astype(jnp.float32), axis=1)
    routed = mixed.astype(jnp.bfloat16)
    residual = (tokens.astype(jnp.float32) + routed.astype(jnp.float32)).astype(jnp.bfloat16)
    logits = jnp.dot(residual, gate_proj, preferred_element_type=jnp.float32).astype(jnp.bfloat16)
    heads_v = head_decay.shape[0]
    heads_k = heads_v // 2
    key_dim = query_in.shape[2] // heads_k
    heads_dev = heads_v // seq_size
    beta_logit = logits[:, :heads_v]
    decay_logit = logits[:, heads_v:]
    queries = query_in[0]
    key_rows = key_in[0]
    values_in = value_in[0]
    inverse_in = block_inverse[0]

    def repeated(values):
        return jnp.repeat(values.reshape(tok_rows, heads_k, key_dim), 2, axis=1).reshape(
            tok_rows, -1
        )

    full_q, full_k, got_v, got_inv, got_beta, got_decay = (
        lax.all_to_all(repeated(queries), "seq", split_axis=1, concat_axis=0, tiled=True),
        lax.all_to_all(repeated(key_rows), "seq", split_axis=1, concat_axis=0, tiled=True),
        lax.all_to_all(values_in, "seq", split_axis=1, concat_axis=0, tiled=True),
        lax.all_to_all(inverse_in, "seq", split_axis=1, concat_axis=0, tiled=True),
        lax.all_to_all(beta_logit, "seq", split_axis=1, concat_axis=0, tiled=True),
        lax.all_to_all(decay_logit, "seq", split_axis=1, concat_axis=0, tiled=True),
    )
    seq_len = full_q.shape[0]
    block_size = inverse_in.shape[1] // heads_v
    block_count = seq_len // block_size
    query_n = normalized(full_q, heads_dev, key_dim ** (-0.5))
    key_n = normalized(full_k, heads_dev, 0.5)

    def arrange(values):
        return values.reshape(block_count, block_size, heads_dev, -1).transpose(2, 0, 1, 3)

    head_start = lax.axis_index("seq") * heads_dev
    decay_rate = jnp.exp(lax.dynamic_slice_in_dim(head_decay, head_start, heads_dev))
    beta_gate = jax.nn.sigmoid(got_beta.astype(jnp.float32))
    decay_log = -decay_rate[None, :] * jax.nn.softplus(got_decay.astype(jnp.float32))
    result = delta_blocks(
        arrange(query_n),
        arrange(key_n),
        arrange(got_v.reshape(seq_len, heads_dev, -1)),
        arrange(got_inv.reshape(seq_len, heads_dev, block_size)),
        beta_gate.reshape(block_count, block_size, heads_dev).transpose(2, 0, 1),
        decay_log.reshape(block_count, block_size, heads_dev).transpose(2, 0, 1),
    )
    flat_out = result.transpose(1, 2, 0, 3).reshape(seq_len, -1)
    core_out = lax.all_to_all(flat_out, "seq", split_axis=0, concat_axis=1, tiled=True)
    return (routed[None], core_out[None])


def solution(mesh):
    in_specs = (
        P("exp", "seq", None),
        P("exp", "seq", None),
        P("exp", "seq", None),
        P("exp", "seq"),
        P(),
        P("exp", "seq", None),
        P("exp", "seq", None),
        P("exp", "seq", None),
        P(),
        P(),
        P("exp", "seq", None),
        P("exp", "seq", None),
        P("exp", "seq", None),
        P("exp", "seq", None),
    )
    out_specs = (P("exp", "seq", None), P("exp", "seq", None))
    return jax.shard_map(
        per_device, mesh=mesh, in_specs=in_specs, out_specs=out_specs, check_vma=False
    )
```

profile of v0, /device:TPU:1, one launch (start us, length us, event | category | flops | bytes accessed | tf_op | source)
XLA Modules:
  0.0 756.7 jit_solution(230179408285907515)
XLA Ops:
  7.9 2.0 copy.125
  10.0 10.4 %all-to-all-start.4 = ((bf16[128,32,64]{0,2,1:T(8,128)(2,1)}), bf16[128,32,64]{0,2,1:T(8,128)(2,1)S(1)}, u32[]{:S(2)}, u32[]{:S(2)}) async-start(bf16[128,32,64]{0,2,1:T(8,128)(2,1)} %bitcast.23), calls=%async_computation.4 | async-start | bytes 1048576 | tf_op jit(solution)/shard_map/all_to_all | solution.py:154
  23.7 8.4 %all-to-all-done.4 = bf16[128,32,64]{0,2,1:T(8,128)(2,1)S(1)} async-done(((bf16[128,32,64]{0,2,1:T(8,128)(2,1)}), bf16[128,32,64]{0,2,1:T(8,128)(2,1)S(1)}, u32[]{:S(2)}, u32[]{:S(2)}) %all-to-all-start.4) | async-done | bytes 524320 | tf_op jit(solution)/shard_map/all_to_all | solution.py:154
  33.4 3.7 all-to-all-start.3
  37.3 3.3 gather_fusion
  40.6 3.2 broadcast_select_fusion
  43.8 10.7 %all-to-all-done.3 = bf16[128,32,128]{2,0,1:T(8,128)(2,1)S(1)} async-done(((bf16[128,32,128]{2,0,1:T(8,128)(2,1)}), bf16[128,32,128]{2,0,1:T(8,128)(2,1)S(1)}, u32[]{:S(2)}, u32[]{:S(2)}) %all-to-all-start.3) | async-done | bytes 1048608 | tf_op jit(solution)/shard_map/all_to_all | solution.py:152
  54.5 12.8 %all-to-all-start = ((bf16[16,32,2048]{2,1,0:T(8,128)(2,1)}), bf16[16,32,2048]{2,1,0:T(8,128)(2,1)}, u32[]{:S(2)}, u32[]{:S(2)}) async-start(bf16[16,32,2048]{2,1,0:T(8,128)(2,1)} %broadcast_select_fusion), calls=%async_computation | async-start | bytes 4194304 | tf_op jit(solution)/shard_map/all_to_all | solution.py:98
  69.1 90.2 %all-to-all-done = bf16[16,32,2048]{2,1,0:T(8,128)(2,1)} async-done(((bf16[16,32,2048]{2,1,0:T(8,128)(2,1)}), bf16[16,32,2048]{2,1,0:T(8,128)(2,1)}, u32[]{:S(2)}, u32[]{:S(2)}) %all-to-all-start) | async-done | bytes 2097184 | tf_op jit(solution)/shard_map/all_to_all | solution.py:98
  160.5 8.1 %all-to-all-start.7 = ((bf16[128,32,128]{2,0,1:T(8,128)(2,1)}), bf16[128,32,128]{2,0,1:T(8,128)(2,1)S(1)}, u32[]{:S(2)}, u32[]{:S(2)}) async-start(bf16[128,32,128]{2,0,1:T(8,128)(2,1)} %bitcast.35), calls=%async_computation.7 | async-start | bytes 2097152 | tf_op jit(solution)/shard_map/all_to_all | solution.py:151
  168.6 3.5 fusion.26
  172.2 38.8 %all-gather.9.cloned.1.call-done = bf16[1,2048,512]{2,1,0:T(8,128)(2,1)} async-done(((bf16[1,64,512]{2,1,0:T(8,128)(2,1)}), bf16[1,2048,512]{2,1,0:T(8,128)(2,1)}) %all-gather.9.cloned.1.call-update) | async-done | bytes 2097168 | tf_op jit(solution)/shard_map/all_gather | solution.py:105
  211.0 6.6 convolution_convert_fusion
  218.6 12.0 %all-to-all-start.1 = ((bf16[16,32,2048]{2,1,0:T(8,128)(2,1)}), bf16[16,32,2048]{2,1,0:T(8,128)(2,1)S(1)}, u32[]{:S(2)}, u32[]{:S(2)}) async-start(bf16[16,32,2048]{2,1,0:T(8,128)(2,1)} %bitcast.187), calls=%async_computation.1 | async-start | bytes 4194304 | tf_op jit(solution)/shard_map/all_to_all | solution.py:113
  237.4 2.3 copy.129
  239.6 2.3 copy.130
  246.2 1.6 copy.126
  247.8 2.7 reshape.556
  250.4 3.0 add_convert_fusion
  253.4 2.9 copy.131
  257.6 65.0 %all-to-all-done.1 = bf16[16,32,2048]{2,1,0:T(8,128)(2,1)S(1)} async-done(((bf16[16,32,2048]{2,1,0:T(8,128)(2,1)}), bf16[16,32,2048]{2,1,0:T(8,128)(2,1)S(1)}, u32[]{:S(2)}, u32[]{:S(2)}) %all-to-all-start.1) | async-done | bytes 2097184 | tf_op jit(solution)/shard_map/all_to_all | solution.py:113
  322.6 6.4 all-to-all-start.6
  329.1 2.4 multiply_reduce_fusion
  331.5 2.5 gather_fusion.1
  334.0 1.8 gather.15
  335.8 4.1 multiply_reduce_fusion.2
  341.7 4.4 all-to-all-done.6
  346.0 4.0 all-to-all-start.2
  351.0 2.8 convert_element_type.352
  353.8 2.9 convert_element_type.350
  357.4 7.4 all-to-all-start.5
  367.3 4.5 all-to-all-done.5
  374.1 3.7 convolution_bitcast_fusion.3
  377.8 2.5 convolution_bitcast_fusion.2
  380.3 3.7 convert_multiply_fusion
  384.0 339.7 %while.15 = (s32[]{:T(128)}, f32[1,128,128]{2,1,0:T(8,128)S(1)}, bf16[64,1,64,128]{3,2,1,0:T(8,128)(2,1)}, f32[64,1,64,128]{3,2,1,0:T(8,128)}, f32[64,1]{0,1:T(1...) while((s32[]{:T(128)}, f32[1,128,128]{2,1,0:T(8,128)S(1)}, ...), condition=%wide.region_11.12_spmd.clone, body=%wide.region_10.11_spmd.clone.sunk | while | flops 27361284 | bytes 461957 | solution.py:56
  384.0 1.6 bitcast_dynamic-update-slice_fusion.2
  431.7 1.6 bitcast_dynamic-update-slice_fusion.2
  458.3 1.6 bitcast_dynamic-update-slice_fusion.2
  479.5 1.6 bitcast_dynamic-update-slice_fusion.2
  516.7 1.6 bitcast_dynamic-update-slice_fusion.2
  543.2 1.6 bitcast_dynamic-update-slice_fusion.2
  622.8 1.6 bitcast_dynamic-update-slice_fusion.2
  654.7 1.6 bitcast_dynamic-update-slice_fusion.2
  704.0 1.6 fusion.81
  713.1 1.6 bitcast_dynamic-update-slice_fusion.2
  723.7 3.9 fusion.22
  727.6 20.6 %all_to_all.104 = bf16[32,128,128]{2,1,0:T(8,128)(2,1)S(1)} all-to-all(bf16[32,128,128]{2,1,0:T(8,128)(2,1)S(1)} %bitcast.184), channel_id=1, replica_groups=mesh['seq'=32,'exp'=16] {'seq'}, dimensions={0} | all-to-all | bytes 2097152 | tf_op jit(solution)/shard_map/all_to_all | solution.py:180
  (357 shorter events, 353.4 us)
Async XLA Ops:
  7.2 333.5 %copy-start = (bf16[2048,64]{0,1:T(8,128)(2,1)S(1)}, bf16[2048,64]{0,1:T(8,128)(2,1)}, u32[]{:S(2)}) copy-start(bf16[2048,64]{0,1:T(8,128)(2,1)} %param.24) | copy-start | bytes 786436
  7.2 13.2 %copy-start.15 = (s32[1,128,2]{1,2,0:T(2,128)S(1)}, s32[1,128,2]{1,2,0:T(2,128)}, u32[]{:S(2)}) copy-start(s32[1,128,2]{1,2,0:T(2,128)} %param.17) | copy-start | bytes 3076
  7.2 14.7 %copy-start.8 = (bf16[1,128,2048]{2,1,0:T(8,128)(2,1)S(1)}, bf16[1,128,2048]{2,1,0:T(8,128)(2,1)}, u32[]{:S(2)}) copy-start(bf16[1,128,2048]{2,1,0:T(8,128)(2,1)} %param.27) | copy-start | bytes 1572868
  7.2 161.4 %all-gather.7.cloned.1.call-start = ((), (), s32[]{:S(2)}) async-start(), calls=%async_computation.9 | async-start | bytes 2162688 | tf_op jit(solution)/shard_map/all_gather | solution.py:104
  10.0 22.2 %all-to-all-start.4 = ((bf16[128,32,64]{0,2,1:T(8,128)(2,1)}), bf16[128,32,64]{0,2,1:T(8,128)(2,1)S(1)}, u32[]{:S(2)}, u32[]{:S(2)}) async-start(bf16[128,32,64]{0,2,1:T(8,128)(2,1)} %bitcast.23), calls=%async_computation.4 | async-start | bytes 1048576 | tf_op jit(solution)/shard_map/all_to_all | solution.py:154
  22.2 15.0 %copy-start.6 = (bf16[1,128,2048]{2,1,0:T(8,128)(2,1)S(1)}, bf16[1,128,2048]{2,1,0:T(8,128)(2,1)}, u32[]{:S(2)}) copy-start(bf16[1,128,2048]{2,1,0:T(8,128)(2,1)} %param.16) | copy-start | bytes 1572868
  22.3 11.1 %copy-start.16 = (s32[256,1]{0,1:T(1,128)}, s32[256,1]{0,1:T(1,128)S(1)}, u32[]{:S(2)}) copy-start(s32[256,1]{0,1:T(1,128)S(1)} %compare_select_fusion.1) | copy-start | bytes 3076
  32.1 1.2 copy-start.4
  33.4 21.1 %all-to-all-start.3 = ((bf16[128,32,128]{2,0,1:T(8,128)(2,1)}), bf16[128,32,128]{2,0,1:T(8,128)(2,1)S(1)}, u32[]{:S(2)}, u32[]{:S(2)}) async-start(bf16[128,32,128]{2,0,1:T(8,128)(2,1)} %bitcast.18), calls=%async_computation.3 | async-start | bytes 2097152 | tf_op jit(solution)/shard_map/all_to_all | solution.py:152
  43.8 25.1 %copy-start.9 = (bf16[1,128,2048]{2,1,0:T(8,128)(2,1)S(1)}, bf16[1,128,2048]{2,1,0:T(8,128)(2,1)}, u32[]{:S(2)}) copy-start(bf16[1,128,2048]{2,1,0:T(8,128)(2,1)} %param.26) | copy-start | bytes 1572868
  54.5 104.8 %all-to-all-start = ((bf16[16,32,2048]{2,1,0:T(8,128)(2,1)}), bf16[16,32,2048]{2,1,0:T(8,128)(2,1)}, u32[]{:S(2)}, u32[]{:S(2)}) async-start(bf16[16,32,2048]{2,1,0:T(8,128)(2,1)} %broadcast_select_fusion), calls=%async_computation | async-start | bytes 4194304 | tf_op jit(solution)/shard_map/all_to_all | solution.py:98
  67.3 104.8 %all-gather.11.cloned.1.call-start = ((), (), s32[]{:S(2)}) async-start(), calls=%async_computation.11 | async-start | bytes 2162688 | tf_op jit(solution)/shard_map/all_gather | solution.py:109
  68.1 142.9 %all-gather.9.cloned.1.call-start = ((), (), s32[]{:S(2)}) async-start(), calls=%async_computation.10 | async-start | bytes 2162688 | tf_op jit(solution)/shard_map/all_gather | solution.py:105
  160.5 57.1 %all-to-all-start.7 = ((bf16[128,32,128]{2,0,1:T(8,128)(2,1)}), bf16[128,32,128]{2,0,1:T(8,128)(2,1)S(1)}, u32[]{:S(2)}, u32[]{:S(2)}) async-start(bf16[128,32,128]{2,0,1:T(8,128)(2,1)} %bitcast.35), calls=%async_computation.7 | async-start | bytes 2097152 | tf_op jit(solution)/shard_map/all_to_all | solution.py:151
  217.6 1.0 copy-start.2
  218.6 104.0 %all-to-all-start.1 = ((bf16[16,32,2048]{2,1,0:T(8,128)(2,1)}), bf16[16,32,2048]{2,1,0:T(8,128)(2,1)S(1)}, u32[]{:S(2)}, u32[]{:S(2)}) async-start(bf16[16,32,2048]{2,1,0:T(8,128)(2,1)} %bitcast.187), calls=%async_computation.1 | async-start | bytes 4194304 | tf_op jit(solution)/shard_map/all_to_all | solution.py:113
  322.6 23.4 %all-to-all-start.6 = ((bf16[128,32,128]{2,0,1:T(8,128)(2,1)}), bf16[128,32,128]{2,0,1:T(8,128)(2,1)}, u32[]{:S(2)}, u32[]{:S(2)}) async-start(bf16[128,32,128]{2,0,1:T(8,128)(2,1)} %copy.130), calls=%async_computation.6 | async-start | bytes 2097152 | tf_op jit(solution)/shard_map/all_to_all | solution.py:153
  334.0 6.7 copy-start.7
  334.0 16.0 %copy-start.12 = (f32[128,32]{0,1:T(8,128)S(1)}, f32[128,32]{0,1:T(8,128)}, u32[]{:S(2)}) copy-start(f32[128,32]{0,1:T(8,128)} %multiply_reduce_fusion) | copy-start | bytes 49156
  334.0 16.0 %copy-start.13 = (f32[32,128]{1,0:T(8,128)S(1)}, f32[32,128]{1,0:T(8,128)}, u32[]{:S(2)}) copy-start(f32[32,128]{1,0:T(8,128)} %multiply_bitcast_fusion.1) | copy-start | bytes 49156
  339.9 0.8 copy-start.5
  346.0 11.3 %all-to-all-start.2 = ((bf16[128,32,1]{0,2,1:T(2,128)(2,1)}), bf16[128,32,1]{0,2,1:T(2,128)(2,1)S(1)}, u32[]{:S(2)}, u32[]{:S(2)}) async-start(bf16[128,32,1]{0,2,1:T(2,128)(2,1)} %copy.123), calls=%async_computation.2 | async-start | bytes 32768 | tf_op jit(solution)/shard_map/all_to_all | solution.py:156
  353.8 20.2 %copy-start.3 = (bf16[64,64,64]{2,1,0:T(8,128)(2,1)S(1)}, bf16[64,64,64]{2,1,0:T(8,128)(2,1)}, u32[]{:S(2)}) copy-start(bf16[64,64,64]{2,1,0:T(8,128)(2,1)} %copy.131) | copy-start | bytes 1572868
  357.4 14.4 %all-to-all-start.5 = ((bf16[128,32,1]{0,2,1:T(2,128)(2,1)}), bf16[128,32,1]{0,2,1:T(2,128)(2,1)}, u32[]{:S(2)}, u32[]{:S(2)}) async-start(bf16[128,32,1]{0,2,1:T(2,128)(2,1)} %copy.127), calls=%async_computation.5 | async-start | bytes 32768 | tf_op jit(solution)/shard_map/all_to_all | solution.py:155
  377.7 2.5 copy-start.1
  377.7 2.5 copy-start.10
  380.3 3.7 copy-start.17
  383.9 339.8 %copy-start.11 = (f32[64,64]{1,0:T(8,128)S(1)}, f32[64,64]{1,0:T(8,128)}, u32[]{:S(2)}) copy-start(f32[64,64]{1,0:T(8,128)} %mul.296) | copy-start | bytes 49156
  383.9 339.8 %copy-start.14 = (pred[64,64]{1,0:T(8,128)(4,1)S(1)}, pred[64,64]{1,0:T(8,128)(4,1)}, u32[]{:S(2)}) copy-start(pred[64,64]{1,0:T(8,128)(4,1)} %iota_compare_fusion.2) | copy-start | bytes 12292
Sparse Core Ops, SparseCore 0:
  11.2 71.9 all-gather.6
  86.3 58.4 all-gather.10
  147.9 63.0 all-gather.8
where the time goes:
time: 772 us; the launch traced here: 757 us
  matrix products  319 us (41%)
  waiting for transfers between devices  224 us (29%)
  local copies, waits for them, and re-layouts  77.4 us (10%)
  starting transfers between devices  65 us (8%)
  other arithmetic  34.6 us (4%)
  blocking collectives  20.6 us (3%)
  between operations  14.9 us (2%)
    dot_general x64, matrix products, advance(): jnp.einsum('hid,hde->hie', mix_now, carry_state, precision=highest)  100 us
    dot_general x64, matrix products, advance(): jnp.einsum('hid,hde->hie', gate_now, carry_state, precision=highest)  99.6 us
    dot_general x64, matrix products, advance(): jnp.einsum('hid,hie->hde', keyd_now, fresh_vals, preferred_element_type=j...  97.4 us
    all_to_all x1, waiting for transfers between devices, per_device(): lax.all_to_all(outgoing, 'exp', split_axis=0, concat_axis=0, tiled=True)  90.2 us
    all_to_all x1, waiting for transfers between devices, per_device(): lax.all_to_all(produced, 'exp', split_axis=0, concat_axis=0, tiled=True)  65 us
    dynamic_slice x64, local copies, waits for them, and re-layouts, delta_blocks(): _, (fresh_vals, early_out) = lax.scan(advance, initial, moved_seq)  41.1 us
    all_gather x1, waiting for transfers between devices, per_device(): up_proj_h = add_rows(lax.all_gather(w_up[0], 'seq', axis=0, tiled=True))  38.8 us
    all_to_all x1, blocking collectives, per_device(): lax.all_to_all(flat_out, 'seq', split_axis=0, concat_axis=1, tiled=True)  20.6 us
  transfers between devices with their start and end apart: 11, of which 7 were waited for; matrix products, arithmetic and copies ran while one was open for 10% of the time, Pallas kernels for 0%

commit v1 on v0

--- a/solution.py
+++ b/solution.py
@@ -1,65 +1,114 @@
+import functools
+
 import jax
 import jax.numpy as jnp
 from jax import lax
+from jax.experimental import pallas as pl
+from jax.experimental.pallas import tpu as pltpu
 from jax.sharding import PartitionSpec as P
 
 highest = lax.Precision.HIGHEST
 
 
-def normalized(values, head_count, factor_scale):
-    flat_vals = values.astype(jnp.float32)
-    shaped = flat_vals.reshape(flat_vals.shape[0], head_count, -1)
-    factor = lax.rsqrt(jnp.sum(shaped * shaped, axis=-1, keepdims=True) + 1e-06) * factor_scale
-    return (shaped * factor).astype(jnp.bfloat16)
-
-
-def delta_blocks(queries, key_rows, values, inverse, beta_gate, decay_log):
-    head_count, block_count, block_size, key_dim = queries.shape
-    value_dim = values.shape[-1]
-    cumulative = jnp.cumsum(decay_log, axis=-1)
-    eye_mat = jnp.eye(block_size, dtype=jnp.float32)
-    strict = jnp.tril(jnp.ones((block_size, block_size), jnp.float32), -1)
-    causal = jnp.tril(jnp.ones((block_size, block_size), jnp.bool_))
-    solver = (eye_mat + strict * inverse.astype(jnp.float32)).astype(jnp.bfloat16)
-    beta_vals = (beta_gate[..., None] * values.astype(jnp.float32)).astype(jnp.bfloat16)
-    beta_keys = (
-        (beta_gate * jnp.exp(cumulative))[..., None] * key_rows.astype(jnp.float32)
-    ).astype(jnp.bfloat16)
-    new_base = jnp.einsum("hnij,hnjd->hnid", solver, beta_vals, preferred_element_type=jnp.float32)
-    key_mix = jnp.einsum("hnij,hnjd->hnid", solver, beta_keys, preferred_element_type=jnp.float32)
-    query_gate = queries.astype(jnp.float32) * jnp.exp(cumulative)[..., None]
-    spread = jnp.where(causal, cumulative[..., :, None] - cumulative[..., None, :], 0.0)
-    scores = jnp.einsum("hnid,hnjd->hnij", queries, key_rows, preferred_element_type=jnp.float32)
-    weights = jnp.where(causal, scores * jnp.exp(spread), 0.0).astype(jnp.bfloat16)
-    tail_decay = jnp.exp(cumulative[..., -1:] - cumulative)
-    key_decay = (key_rows.astype(jnp.float32) * tail_decay[..., None]).astype(jnp.bfloat16)
-    carry_decay = jnp.exp(cumulative[..., -1])
-
-    def advance(carry_state, inputs):
-        mix_now, base_now, gate_now, keyd_now, keep_now = inputs
-        fresh_vals = (
-            base_now - jnp.einsum("hid,hde->hie", mix_now, carry_state, precision=highest)
+def delta_kernel(block_size, q_ref, k_ref, v_ref, inv_ref, gate_ref, rate_ref, out_ref, state_ref, beta_ref, cum_ref):
+    step = pl.program_id(0)
+    chunk_rows, key_dim = q_ref.shape
+    per_chunk = chunk_rows // block_size
+    rows_i = lax.broadcasted_iota(jnp.int32, (block_size, block_size), 0)
+    cols_i = lax.broadcasted_iota(jnp.int32, (block_size, block_size), 1)
+    diagonal = rows_i == cols_i
+    below = rows_i > cols_i
+    causal = rows_i >= cols_i
+
+    @pl.when(step == 0)
+    def _():
+        state_ref[...] = jnp.zeros_like(state_ref)
+        beta_ref[...] = jax.nn.sigmoid(gate_ref[0].astype(jnp.float32))
+        raw = gate_ref[1].astype(jnp.float32)
+        soft = jnp.maximum(raw, 0.0) + jnp.log1p(jnp.exp(-jnp.abs(raw)))
+        log_decay = -jnp.exp(rate_ref[0, 0]) * soft
+        upper = (rows_i <= cols_i).astype(jnp.float32)
+        cum_ref[...] = jnp.dot(
+            log_decay, upper, precision=highest, preferred_element_type=jnp.float32
+        )
+
+    def dot(a, b, contract):
+        return lax.dot_general(
+            a, b, ((contract[:1], contract[1:]), ((), ())), preferred_element_type=jnp.float32
+        )
+
+    def column(row):
+        return jnp.sum(jnp.where(diagonal, row, 0.0), axis=1, keepdims=True)
+
+    def normal(values, scale):
+        vals = values.astype(jnp.float32)
+        factor = lax.rsqrt(jnp.sum(vals * vals, axis=1, keepdims=True) + 1e-06) * scale
+        return (vals * factor).astype(jnp.bfloat16)
+
+    state = state_ref[...]
+    for piece in range(per_chunk):
+        span = pl.ds(piece * block_size, block_size)
+        block = step * per_chunk + piece
+        cum_row = cum_ref[pl.ds(block, 1), :]
+        cum_col = column(cum_row)
+        beta_col = column(beta_ref[pl.ds(block, 1), :])
+        last = cum_row[:, block_size - 1 :]
+        grow = jnp.exp(cum_col)
+        query_n = normal(q_ref[span, :], key_dim ** (-0.5))
+        key_n = normal(k_ref[span, :], 0.5)
+        key_f = key_n.astype(jnp.float32)
+        solver = jnp.where(
+            diagonal, 1.0, jnp.where(below, inv_ref[span, :].astype(jnp.float32), 0.0)
         ).astype(jnp.bfloat16)
-        early_out = jnp.einsum("hid,hde->hie", gate_now, carry_state, precision=highest)
-        carry_state = keep_now[:, None, None] * carry_state + jnp.einsum(
-            "hid,hie->hde", keyd_now, fresh_vals, preferred_element_type=jnp.float32
-        )
-        return (carry_state, (fresh_vals, early_out))
-
-    moved_seq = tuple(
-        (
-            jnp.moveaxis(element, 1, 0)
-            for element in (key_mix, new_base, query_gate, key_decay, carry_decay)
-        )
-    )
-    initial = jnp.zeros((head_count, key_dim, value_dim), jnp.float32)
-    _, (fresh_vals, early_out) = lax.scan(advance, initial, moved_seq)
-    fresh_vals = jnp.moveaxis(fresh_vals, 0, 1)
-    early_out = jnp.moveaxis(early_out, 0, 1)
-    local_out = jnp.einsum(
-        "hnij,hnjd->hnid", weights, fresh_vals, preferred_element_type=jnp.float32
-    )
-    return (early_out + local_out).astype(jnp.bfloat16)
+        beta_vals = (beta_col * v_ref[span, :].astype(jnp.float32)).astype(jnp.bfloat16)
+        beta_keys = ((beta_col * grow) * key_f).astype(jnp.bfloat16)
+        new_base = dot(solver, beta_vals, (1, 0))
+        key_mix = dot(solver, beta_keys, (1, 0)).astype(jnp.bfloat16)
+        query_gate = (query_n.astype(jnp.float32) * grow).astype(jnp.bfloat16)
+        spread = jnp.exp(jnp.where(causal, cum_col - cum_row, 0.0))
+        weights = jnp.where(causal, dot(query_n, key_n, (1, 1)) * spread, 0.0).astype(jnp.bfloat16)
+        key_decay = (key_f * jnp.exp(last - cum_col)).astype(jnp.bfloat16)
+        erase = dot(key_mix, key_decay, (0, 0)).astype(jnp.bfloat16)
+        write = dot(new_base.astype(jnp.bfloat16), key_decay, (0, 0))
+        held = state.astype(jnp.bfloat16)
+        fresh = (new_base - dot(key_mix, held, (1, 1))).astype(jnp.bfloat16)
+        out_ref[span, :] = (dot(query_gate, held, (1, 1)) + dot(weights, fresh, (1, 0))).astype(
+            jnp.bfloat16
+        )
+        state = jnp.exp(last) * state + (write - dot(held, erase, (1, 0)))
+    state_ref[...] = state
+
+
+def delta_rule(queries, key_rows, values, inverse, gates, rate):
+    seq_len, key_dim = queries.shape
+    value_dim = values.shape[1]
+    block_size = inverse.shape[1]
+    block_count = seq_len // block_size
+    chunk = 8 * block_size
+
+    def rows(width):
+        return pl.BlockSpec((chunk, width), lambda i: (i, 0))
+
+    return pl.pallas_call(
+        functools.partial(delta_kernel, block_size),
+        grid=(seq_len // chunk,),
+        out_shape=jax.ShapeDtypeStruct((seq_len, value_dim), jnp.bfloat16),
+        in_specs=[
+            rows(key_dim),
+            rows(key_dim),
+            rows(value_dim),
+            rows(block_size),
+            pl.BlockSpec((2, block_count, block_size), lambda i: (0, 0, 0)),
+            pl.BlockSpec((1, 1), lambda i: (0, 0), memory_space=pltpu.SMEM),
+        ],
+        out_specs=rows(value_dim),
+        scratch_shapes=[
+            pltpu.VMEM((value_dim, key_dim), jnp.float32),
+            pltpu.VMEM((block_count, block_size), jnp.float32),
+            pltpu.VMEM((block_count, block_size), jnp.float32),
+        ],
+        name="delta_rule",
+    )(queries, key_rows, values, inverse, gates, rate)
 
 
 def per_device(
@@ -158,25 +207,10 @@
     seq_len = full_q.shape[0]
     block_size = inverse_in.shape[1] // heads_v
     block_count = seq_len // block_size
-    query_n = normalized(full_q, heads_dev, key_dim ** (-0.5))
-    key_n = normalized(full_k, heads_dev, 0.5)
-
-    def arrange(values):
-        return values.reshape(block_count, block_size, heads_dev, -1).transpose(2, 0, 1, 3)
-
     head_start = lax.axis_index("seq") * heads_dev
-    decay_rate = jnp.exp(lax.dynamic_slice_in_dim(head_decay, head_start, heads_dev))
-    beta_gate = jax.nn.sigmoid(got_beta.astype(jnp.float32))
-    decay_log = -decay_rate[None, :] * jax.nn.softplus(got_decay.astype(jnp.float32))
-    result = delta_blocks(
-        arrange(query_n),
-        arrange(key_n),
-        arrange(got_v.reshape(seq_len, heads_dev, -1)),
-        arrange(got_inv.reshape(seq_len, heads_dev, block_size)),
-        beta_gate.reshape(block_count, block_size, heads_dev).transpose(2, 0, 1),
-        decay_log.reshape(block_count, block_size, heads_dev).transpose(2, 0, 1),
-    )
-    flat_out = result.transpose(1, 2, 0, 3).reshape(seq_len, -1)
+    rate = lax.dynamic_slice_in_dim(head_decay, head_start, heads_dev).reshape(1, 1)
+    gates = jnp.stack([got_beta, got_decay]).reshape(2, block_count, block_size)
+    flat_out = delta_rule(full_q, full_k, got_v, got_inv, gates, rate)
     core_out = lax.all_to_all(flat_out, "seq", split_axis=0, concat_axis=1, tiled=True)
     return (routed[None], core_out[None])
 

time: 772 us -> 440 us (0.57); the launches traced: 757 us -> 438 us
  matrix products: 319 us -> 10.6 us
  local copies, waits for them, and re-layouts: 77.4 us -> 23.4 us
  waiting for transfers between devices: 224 us -> 271 us
  Pallas kernels: 0 us -> 29.4 us
  other arithmetic: 34.6 us -> 7.24 us
    dot_general x195 -> x0, matrix products: 307 us -> none  [the longest x64 100 us: advance(): jnp.einsum('hid,hde->hie', mix_now, carry_state, precision=highest)]
    dynamic_slice x65 -> x1, local copies, waits for them, and re-layouts: 42.3 us -> 0.56 us  [per_device(): lax.dynamic_slice_in_dim(head_decay, head_start, heads_dev).reshape(1, 1)]
    pallas_call x0 -> x1, Pallas kernels: none -> 29.4 us  [delta_rule(): pl.pallas_call(functools.partial(delta_kernel, block_size), grid=(seq_len...]
    all_to_all x1, waiting for transfers between devices: 65 us -> 90.9 us  [per_device(): lax.all_to_all(produced, 'exp', split_axis=0, concat_axis=0, tiled=True)]
    convert_element_type x7 -> x0, other arithmetic: 10.8 us -> none  [the longest x2 3.05 us: normalized(): flat_vals = values.astype(jnp.float32)]
    all_gather x1, waiting for transfers between devices: 38.8 us -> 48.8 us  [per_device(): up_proj_h = add_rows(lax.all_gather(w_up[0], 'seq', axis=0, tiled=True))]
    all_to_all x1, waiting for transfers between devices: 4.37 us -> 14.2 us  [per_device(): lax.all_to_all(values_in, 'seq', split_axis=1, concat_axis=0, tiled=True)]
  transfers between devices with their start and end apart: 11 -> 11, of which waited for: 7 -> 8; matrix products, arithmetic and copies ran while one was open for 10% -> 8% of each run, Pallas kernels for 0% -> 0%
where the time goes in v1:
time: 440 us; the launch traced here: 438 us
  waiting for transfers between devices  271 us (62%)
  starting transfers between devices  61.2 us (14%)
  Pallas kernels  29.4 us (7%)
  local copies, waits for them, and re-layouts  23.4 us (5%)
  blocking collectives  20.8 us (5%)
  between operations  14.2 us (3%)
  matrix products  10.6 us (2%)
  other arithmetic  7.24 us (2%)
    all_to_all x1, waiting for transfers between devices, per_device(): lax.all_to_all(produced, 'exp', split_axis=0, concat_axis=0, tiled=True)  90.9 us
    all_to_all x1, waiting for transfers between devices, per_device(): lax.all_to_all(outgoing, 'exp', split_axis=0, concat_axis=0, tiled=True)  89.7 us
    all_gather x1, waiting for transfers between devices, per_device(): up_proj_h = add_rows(lax.all_gather(w_up[0], 'seq', axis=0, tiled=True))  48.8 us
    pallas_call x1, Pallas kernels, delta_rule(): pl.pallas_call(functools.partial(delta_kernel, block_size), grid=(seq_len...  29.4 us
    all_to_all x1, blocking collectives, per_device(): lax.all_to_all(flat_out, 'seq', split_axis=0, concat_axis=1, tiled=True)  20.8 us
    all_to_all x1, waiting for transfers between devices, per_device(): lax.all_to_all(values_in, 'seq', split_axis=1, concat_axis=0, tiled=True)  14.2 us
    all_to_all x1, starting transfers between devices, per_device(): lax.all_to_all(outgoing, 'exp', split_axis=0, concat_axis=0, tiled=True)  13 us
    all_to_all x1, starting transfers between devices, per_device(): lax.all_to_all(produced, 'exp', split_axis=0, concat_axis=0, tiled=True)  12 us
  transfers between devices with their start and end apart: 11, of which 8 were waited for; matrix products, arithmetic and copies ran while one was open for 8% of the time, Pallas kernels for 0%

profile of v1, /device:TPU:1, one launch (start us, length us, event | category | flops | bytes accessed | tf_op | source)
XLA Modules:
  0.0 438.2 jit_solution(17747568851901190727)
XLA Ops:
  7.2 0.7 all-gather.7.cloned.1.call-update
  7.9 2.0 copy.93
  10.0 10.4 %all-to-all-start.5 = ((bf16[128,32,64]{0,2,1:T(8,128)(2,1)}), bf16[128,32,64]{0,2,1:T(8,128)(2,1)S(1)}, u32[]{:S(2)}, u32[]{:S(2)}) async-start(bf16[128,32,64]{0,2,1:T(8,128)(2,1)} %bitcast.23), calls=%async_computation.5 | async-start | bytes 1048576 | tf_op jit(solution)/shard_map/all_to_all | solution.py:203
  20.8 0.6 reduce-window.6
  22.0 1.4 scatter_custom_fusion
  23.6 2.5 gather_fusion
  26.1 1.6 broadcast_select_fusion
  27.7 4.5 %all-to-all-done.5 = bf16[128,32,64]{0,2,1:T(8,128)(2,1)S(1)} async-done(((bf16[128,32,64]{0,2,1:T(8,128)(2,1)}), bf16[128,32,64]{0,2,1:T(8,128)(2,1)S(1)}, u32[]{:S(2)}, u32[]{:S(2)}) %all-to-all-start.5) | async-done | bytes 524320 | tf_op jit(solution)/shard_map/all_to_all | solution.py:203
  32.1 0.8 copy-done.3
  33.0 13.0 %all-to-all-start = ((bf16[16,32,2048]{2,1,0:T(8,128)(2,1)}), bf16[16,32,2048]{2,1,0:T(8,128)(2,1)S(1)}, u32[]{:S(2)}, u32[]{:S(2)}) async-start(bf16[16,32,2048]{2,1,0:T(8,128)(2,1)} %broadcast_select_fusion), calls=%async_computation | async-start | bytes 4194304 | tf_op jit(solution)/shard_map/all_to_all | solution.py:147
  46.0 0.7 all-gather.11.cloned.1.call-update
  46.7 0.7 all-gather.9.cloned.1.call-update
  47.4 1.1 copy.99
  48.7 89.7 %all-to-all-done = bf16[16,32,2048]{2,1,0:T(8,128)(2,1)S(1)} async-done(((bf16[16,32,2048]{2,1,0:T(8,128)(2,1)}), bf16[16,32,2048]{2,1,0:T(8,128)(2,1)S(1)}, u32[]{:S(2)}, u32[]{:S(2)}) %all-to-all-start) | async-done | bytes 2097184 | tf_op jit(solution)/shard_map/all_to_all | solution.py:147
  138.4 1.2 broadcast_in_dim.52
  139.6 7.1 %all-to-all-start.2 = ((bf16[128,32,128]{2,0,1:T(8,128)(2,1)}), bf16[128,32,128]{2,0,1:T(8,128)(2,1)S(1)}, u32[]{:S(2)}, u32[]{:S(2)}) async-start(bf16[128,32,128]{2,0,1:T(8,128)(2,1)} %bitcast.15), calls=%async_computation.2 | async-start | bytes 2097152 | tf_op jit(solution)/shard_map/all_to_all | solution.py:200
  146.8 3.8 fusion.3
  150.6 48.8 %all-gather.9.cloned.1.call-done = bf16[1,2048,512]{2,1,0:T(8,128)(2,1)} async-done(((bf16[1,64,512]{2,1,0:T(8,128)(2,1)}), bf16[1,2048,512]{2,1,0:T(8,128)(2,1)}) %all-gather.9.cloned.1.call-update) | async-done | bytes 2097168 | tf_op jit(solution)/shard_map/all_gather | solution.py:154
  199.4 6.3 %convolution_convert_fusion = bf16[512,2048]{1,0:T(8,128)(2,1)} fusion(bf16[1,512,2048]{2,1,0:T(8,128)(2,1)} %all-gather.11.cloned.1.call-done, bf16[512,2048]{1,0:T(8,128)(2,1)S(1)} %bitcast.101, bf16[1,2048,512]{2,1,0:T(8,128)(2,1)} %all-gather.9.cloned.1.call-done, f32[512,512]{1,0:T(8,128)} %fusion.3), kind=kOutput, calls=%fused_computation.3 | convolution fusion | flops 2150105088 | bytes 9437184 | tf_op jit(solution)/shard_map/dot_general | solution.py:156
  205.7 1.0 copy-done.1
  206.7 12.0 %all-to-all-start.1 = ((bf16[16,32,2048]{2,1,0:T(8,128)(2,1)}), bf16[16,32,2048]{2,1,0:T(8,128)(2,1)S(1)}, u32[]{:S(2)}, u32[]{:S(2)}) async-start(bf16[16,32,2048]{2,1,0:T(8,128)(2,1)} %bitcast.102), calls=%async_computation.1 | async-start | bytes 4194304 | tf_op jit(solution)/shard_map/all_to_all | solution.py:162
  219.5 0.2 fusion.15
  219.7 90.9 %all-to-all-done.1 = bf16[16,32,2048]{2,1,0:T(8,128)(2,1)S(1)} async-done(((bf16[16,32,2048]{2,1,0:T(8,128)(2,1)}), bf16[16,32,2048]{2,1,0:T(8,128)(2,1)S(1)}, u32[]{:S(2)}, u32[]{:S(2)}) %all-to-all-start.1) | async-done | bytes 2097184 | tf_op jit(solution)/shard_map/all_to_all | solution.py:162
  310.7 1.2 broadcast_in_dim.53
  311.9 6.3 %all-to-all-start.3 = ((bf16[128,32,128]{2,0,1:T(8,128)(2,1)}), bf16[128,32,128]{2,0,1:T(8,128)(2,1)}, u32[]{:S(2)}, u32[]{:S(2)}) async-start(bf16[128,32,128]{2,0,1:T(8,128)(2,1)} %bitcast.18), calls=%async_computation.3 | async-start | bytes 2097152 | tf_op jit(solution)/shard_map/all_to_all | solution.py:201
  318.5 1.4 gather_fusion.1
  319.8 0.7 gather.15
  320.6 4.1 multiply_reduce_fusion
  324.7 0.3 convolution_convert_fusion.1
  325.0 0.6 copy.96
  325.7 9.5 %all-to-all-done.3 = bf16[128,32,128]{2,0,1:T(8,128)(2,1)} async-done(((bf16[128,32,128]{2,0,1:T(8,128)(2,1)}), bf16[128,32,128]{2,0,1:T(8,128)(2,1)}, u32[]{:S(2)}, u32[]{:S(2)}) %all-to-all-start.3) | async-done | bytes 1048608 | tf_op jit(solution)/shard_map/all_to_all | solution.py:201
  335.1 4.0 all-to-all-start.7
  339.1 0.6 copy.95
  339.7 6.3 %all-to-all-done.7 = bf16[128,32,1]{0,2,1:T(2,128)(2,1)S(1)} async-done(((bf16[128,32,1]{0,2,1:T(2,128)(2,1)}), bf16[128,32,1]{0,2,1:T(2,128)(2,1)S(1)}, u32[]{:S(2)}, u32[]{:S(2)}) %all-to-all-start.7) | async-done | bytes 8224 | tf_op jit(solution)/shard_map/all_to_all | solution.py:205
  346.0 4.1 all-to-all-start.6
  350.2 0.2 copy.101
  350.5 1.4 copy.92
  351.8 5.4 %all-to-all-done.6 = bf16[128,32,1]{0,2,1:T(2,128)(2,1)S(1)} async-done(((bf16[128,32,1]{0,2,1:T(2,128)(2,1)}), bf16[128,32,1]{0,2,1:T(2,128)(2,1)S(1)}, u32[]{:S(2)}, u32[]{:S(2)}) %all-to-all-start.6) | async-done | bytes 8224 | tf_op jit(solution)/shard_map/all_to_all | solution.py:204
  357.2 4.2 all-to-all-start.4
  361.5 0.6 dynamic_slice.3
  362.0 1.4 copy.94
  363.7 0.6 pad_maximum_fusion.gate_ref
  364.3 14.2 %all-to-all-done.4 = bf16[128,32,128]{2,0,1:T(8,128)(2,1)S(1)} async-done(((bf16[128,32,128]{2,0,1:T(8,128)(2,1)}), bf16[128,32,128]{2,0,1:T(8,128)(2,1)S(1)}, u32[]{:S(2)}, u32[]{:S(2)}) %all-to-all-start.4) | async-done | bytes 1048608 | tf_op jit(solution)/shard_map/all_to_all | solution.py:202
  378.5 1.0 copy-done.2
  379.4 29.4 %delta_rule.1 = bf16[4096,128]{1,0:T(8,128)(2,1)} custom-call(bf16[4096,128]{1,0:T(8,128)(2,1)} %bitcast.95, bf16[4096,128]{1,0:T(8,128)(2,1)} %bitcast.20.k_ref, bf16[4096,128]{1,0:T(8,128)(2,1)} %bitcast.96, bf16[4096,64]{1,0:T(8,128)(2,1)} %bitcast.97, bf16[2,64,64]{2,1,0:T(8,128)(2,1)} %pad_maximum_fusion.gate_ref, f32[1,1]{1,0:T(1,128)} %bitcast.30.rate_ref), custom_call_target="tpu_custom_call" | custom-call | tf_op jit(solution)/shard_map/delta_rule/pallas_call | solution.py:92
  408.8 20.8 %all_to_all.134 = bf16[32,128,128]{2,1,0:T(8,128)(2,1)S(1)} all-to-all(bf16[32,128,128]{2,1,0:T(8,128)(2,1)} %bitcast.98), channel_id=1, replica_groups=mesh['seq'=32,'exp'=16] {'seq'}, dimensions={0} | all-to-all | bytes 2097152 | tf_op jit(solution)/shard_map/all_to_all | solution.py:214
  429.7 0.7 copy.97
  430.4 1.3 broadcast_in_dim.54
  (68 shorter events, 2.8 us)
Async XLA Ops:
  7.2 317.5 %copy-start = (bf16[2048,64]{0,1:T(8,128)(2,1)S(1)}, bf16[2048,64]{0,1:T(8,128)(2,1)}, u32[]{:S(2)}) copy-start(bf16[2048,64]{0,1:T(8,128)(2,1)} %param.22) | copy-start | bytes 786436
  7.2 13.2 %copy-start.10 = (s32[1,128,2]{1,2,0:T(2,128)S(1)}, s32[1,128,2]{1,2,0:T(2,128)}, u32[]{:S(2)}) copy-start(s32[1,128,2]{1,2,0:T(2,128)} %param.15) | copy-start | bytes 3076
  7.2 16.3 %copy-start.6 = (bf16[1,128,2048]{2,1,0:T(8,128)(2,1)S(1)}, bf16[1,128,2048]{2,1,0:T(8,128)(2,1)}, u32[]{:S(2)}) copy-start(bf16[1,128,2048]{2,1,0:T(8,128)(2,1)} %param.14) | copy-start | bytes 1572868
  7.2 139.6 %all-gather.7.cloned.1.call-start = ((), (), s32[]{:S(2)}) async-start(), calls=%async_computation.9 | async-start | bytes 2162688 | tf_op jit(solution)/shard_map/all_gather | solution.py:153
  10.0 22.2 %all-to-all-start.5 = ((bf16[128,32,64]{0,2,1:T(8,128)(2,1)}), bf16[128,32,64]{0,2,1:T(8,128)(2,1)S(1)}, u32[]{:S(2)}, u32[]{:S(2)}) async-start(bf16[128,32,64]{0,2,1:T(8,128)(2,1)} %bitcast.23), calls=%async_computation.5 | async-start | bytes 1048576 | tf_op jit(solution)/shard_map/all_to_all | solution.py:203
  32.1 0.8 copy-start.3
  33.0 105.4 %all-to-all-start = ((bf16[16,32,2048]{2,1,0:T(8,128)(2,1)}), bf16[16,32,2048]{2,1,0:T(8,128)(2,1)S(1)}, u32[]{:S(2)}, u32[]{:S(2)}) async-start(bf16[16,32,2048]{2,1,0:T(8,128)(2,1)} %broadcast_select_fusion), calls=%async_computation | async-start | bytes 4194304 | tf_op jit(solution)/shard_map/all_to_all | solution.py:147
  45.9 104.7 %all-gather.11.cloned.1.call-start = ((), (), s32[]{:S(2)}) async-start(), calls=%async_computation.11 | async-start | bytes 2162688 | tf_op jit(solution)/shard_map/all_gather | solution.py:158
  46.7 152.7 %all-gather.9.cloned.1.call-start = ((), (), s32[]{:S(2)}) async-start(), calls=%async_computation.10 | async-start | bytes 2162688 | tf_op jit(solution)/shard_map/all_gather | solution.py:154
  139.6 66.1 %all-to-all-start.2 = ((bf16[128,32,128]{2,0,1:T(8,128)(2,1)}), bf16[128,32,128]{2,0,1:T(8,128)(2,1)S(1)}, u32[]{:S(2)}, u32[]{:S(2)}) async-start(bf16[128,32,128]{2,0,1:T(8,128)(2,1)} %bitcast.15), calls=%async_computation.2 | async-start | bytes 2097152 | tf_op jit(solution)/shard_map/all_to_all | solution.py:200
  205.7 1.0 copy-start.1
  205.7 13.2 %copy-start.9 = (bf16[1,128,2048]{2,1,0:T(8,128)(2,1)S(1)}, bf16[1,128,2048]{2,1,0:T(8,128)(2,1)}, u32[]{:S(2)}) copy-start(bf16[1,128,2048]{2,1,0:T(8,128)(2,1)} %param.25) | copy-start | bytes 1572868
  206.7 104.0 %all-to-all-start.1 = ((bf16[16,32,2048]{2,1,0:T(8,128)(2,1)}), bf16[16,32,2048]{2,1,0:T(8,128)(2,1)S(1)}, u32[]{:S(2)}, u32[]{:S(2)}) async-start(bf16[16,32,2048]{2,1,0:T(8,128)(2,1)} %bitcast.102), calls=%async_computation.1 | async-start | bytes 4194304 | tf_op jit(solution)/shard_map/all_to_all | solution.py:162
  218.7 0.7 copy-start.11
  218.7 0.8 copy-start.13
  218.7 1.0 copy-start.12
  311.9 23.2 %all-to-all-start.3 = ((bf16[128,32,128]{2,0,1:T(8,128)(2,1)}), bf16[128,32,128]{2,0,1:T(8,128)(2,1)}, u32[]{:S(2)}, u32[]{:S(2)}) async-start(bf16[128,32,128]{2,0,1:T(8,128)(2,1)} %bitcast.18), calls=%async_computation.3 | async-start | bytes 2097152 | tf_op jit(solution)/shard_map/all_to_all | solution.py:201
  319.8 4.9 %copy-start.7 = (bf16[1,128,2048]{2,1,0:T(8,128)(2,1)S(1)}, bf16[1,128,2048]{2,1,0:T(8,128)(2,1)}, u32[]{:S(2)}) copy-start(bf16[1,128,2048]{2,1,0:T(8,128)(2,1)} %param.14) | copy-start | bytes 1572868
  320.6 29.6 %copy-start.8 = (bf16[1,128,4096]{2,1,0:T(8,128)(2,1)S(1)}, bf16[1,128,4096]{2,1,0:T(8,128)(2,1)}, u32[]{:S(2)}) copy-start(bf16[1,128,4096]{2,1,0:T(8,128)(2,1)} %param.26) | copy-start | bytes 3145732
  324.7 27.1 %copy-start.5 = (bf16[128,2048]{1,0:T(8,128)(2,1)}, bf16[128,2048]{1,0:T(8,128)(2,1)S(1)}, u32[]{:S(2)}) copy-start(bf16[128,2048]{1,0:T(8,128)(2,1)S(1)} %multiply_reduce_fusion) | copy-start | bytes 1572868
  335.1 10.9 %all-to-all-start.7 = ((bf16[128,32,1]{0,2,1:T(2,128)(2,1)}), bf16[128,32,1]{0,2,1:T(2,128)(2,1)S(1)}, u32[]{:S(2)}, u32[]{:S(2)}) async-start(bf16[128,32,1]{0,2,1:T(2,128)(2,1)} %copy.96), calls=%async_computation.7 | async-start | bytes 32768 | tf_op jit(solution)/shard_map/all_to_all | solution.py:205
  346.0 11.2 %all-to-all-start.6 = ((bf16[128,32,1]{0,2,1:T(2,128)(2,1)}), bf16[128,32,1]{0,2,1:T(2,128)(2,1)S(1)}, u32[]{:S(2)}, u32[]{:S(2)}) async-start(bf16[128,32,1]{0,2,1:T(2,128)(2,1)} %copy.95), calls=%async_computation.6 | async-start | bytes 32768 | tf_op jit(solution)/shard_map/all_to_all | solution.py:204
  350.4 11.0 %copy-start.14 = (f32[32]{0:T(128)S(1)}, f32[32]{0:T(128)}, u32[]{:S(2)}) copy-start(f32[32]{0:T(128)} %param.23) | copy-start | bytes 388
  350.4 11.6 %copy-start.4 = (bf16[128,32,64]{0,2,1:T(8,128)(2,1)S(1)}, bf16[128,32,64]{0,2,1:T(8,128)(2,1)}, u32[]{:S(2)}) copy-start(bf16[128,32,64]{0,2,1:T(8,128)(2,1)} %copy-done.3) | copy-start | bytes 1572868
  357.2 21.2 %all-to-all-start.4 = ((bf16[128,32,128]{2,0,1:T(8,128)(2,1)}), bf16[128,32,128]{2,0,1:T(8,128)(2,1)S(1)}, u32[]{:S(2)}, u32[]{:S(2)}) async-start(bf16[128,32,128]{2,0,1:T(8,128)(2,1)} %copy.92), calls=%async_computation.4 | async-start | bytes 2097152 | tf_op jit(solution)/shard_map/all_to_all | solution.py:202
  378.5 1.0 copy-start.2
Sparse Core Ops, SparseCore 0:
  11.2 64.8 all-gather.6
  79.2 58.4 all-gather.10
  140.9 58.4 all-gather.8

commit v2 on v1

--- a/solution.py
+++ b/solution.py
@@ -31,6 +31,8 @@
         cum_ref[...] = jnp.dot(
             log_decay, upper, precision=highest, preferred_element_type=jnp.float32
         )
+
+    odd = lax.rem(lax.axis_index("seq"), 2) == 1
 
     def dot(a, b, contract):
         return lax.dot_general(
@@ -57,9 +59,9 @@
         query_n = normal(q_ref[span, :], key_dim ** (-0.5))
         key_n = normal(k_ref[span, :], 0.5)
         key_f = key_n.astype(jnp.float32)
-        solver = jnp.where(
-            diagonal, 1.0, jnp.where(below, inv_ref[span, :].astype(jnp.float32), 0.0)
-        ).astype(jnp.bfloat16)
+        both = inv_ref[span, :].astype(jnp.float32)
+        inverse = jnp.where(odd, both[:, block_size:], both[:, :block_size])
+        solver = jnp.where(diagonal, 1.0, jnp.where(below, inverse, 0.0)).astype(jnp.bfloat16)
         beta_vals = (beta_col * v_ref[span, :].astype(jnp.float32)).astype(jnp.bfloat16)
         beta_keys = ((beta_col * grow) * key_f).astype(jnp.bfloat16)
         new_base = dot(solver, beta_vals, (1, 0))
@@ -82,7 +84,7 @@
 def delta_rule(queries, key_rows, values, inverse, gates, rate):
     seq_len, key_dim = queries.shape
     value_dim = values.shape[1]
-    block_size = inverse.shape[1]
+    block_size = inverse.shape[1] // 2
     block_count = seq_len // block_size
     chunk = 8 * block_size
 
@@ -97,7 +99,7 @@
             rows(key_dim),
             rows(key_dim),
             rows(value_dim),
-            rows(block_size),
+            rows(2 * block_size),
             pl.BlockSpec((2, block_count, block_size), lambda i: (0, 0, 0)),
             pl.BlockSpec((1, 1), lambda i: (0, 0), memory_space=pltpu.SMEM),
         ],
@@ -109,6 +111,249 @@
         ],
         name="delta_rule",
     )(queries, key_rows, values, inverse, gates, rate)
+
+
+MESH = pl.DeviceIdType.MESH
+
+
+def greet(exp_peers, seq_peers):
+    exp_size, seq_size = lax.axis_size("exp"), lax.axis_size("seq")
+    exp_me, seq_me = lax.axis_index("exp"), lax.axis_index("seq")
+    barrier = pltpu.get_barrier_semaphore()
+
+    @pl.loop(1, exp_size)
+    def _(r):
+        pl.semaphore_signal(
+            barrier, inc=1, device_id=(seq_me, lax.rem(exp_me + r, exp_size)), device_id_type=MESH
+        )
+
+    for first, count, place in seq_peers:
+
+        @pl.loop(first, first + count)
+        def _(r):
+            pl.semaphore_signal(barrier, inc=1, device_id=(place(r), exp_me), device_id_type=MESH)
+
+    pl.semaphore_wait(barrier, exp_peers + sum(count for _, count, _ in seq_peers))
+
+
+def along_exp(rows_ref, landed_ref, send_sem, recv_sem):
+    exp_size = lax.axis_size("exp")
+    exp_me, seq_me = lax.axis_index("exp"), lax.axis_index("seq")
+
+    def block(r):
+        other = lax.rem(exp_me + r, exp_size)
+        return pltpu.make_async_remote_copy(
+            src_ref=rows_ref.at[other],
+            dst_ref=landed_ref.at[exp_me],
+            send_sem=send_sem.at[r],
+            recv_sem=recv_sem.at[r],
+            device_id=(seq_me, other),
+            device_id_type=MESH,
+        )
+
+    own = pltpu.make_async_copy(rows_ref.at[exp_me], landed_ref.at[exp_me], send_sem.at[0])
+    return block, own
+
+
+def dispatch_kernel(
+    rows_ref, wg_ref, wu_ref, wd_ref, landed_ref, full_g, full_u, full_d,
+    send_sem, recv_sem, own_sem, wsend, wrecv, psend, precv,
+):
+    exp_size, seq_size = lax.axis_size("exp"), lax.axis_size("seq")
+    exp_me, seq_me = lax.axis_index("exp"), lax.axis_index("seq")
+    chips = seq_size // 2
+    chip, core = seq_me // 2, lax.rem(seq_me, 2)
+    partner = chip * 2 + 1 - core
+
+    def same_core(r):
+        return lax.rem(chip + r, chips) * 2 + core
+
+    greet(exp_size - 1, ((1, chips - 1, same_core), (0, 1, lambda r: partner)))
+    block, own = along_exp(rows_ref, landed_ref, send_sem, recv_sem)
+    pairs = ((wg_ref, full_g), (wu_ref, full_u), (wd_ref, full_d))
+
+    def slot(full, shard, who):
+        depth = shard.shape[0]
+        return full.at[pl.ds(pl.multiple_of(who * depth, depth), depth)]
+
+    def spread(i, r):
+        shard, full = pairs[i]
+        return pltpu.make_async_remote_copy(
+            src_ref=shard,
+            dst_ref=slot(full, shard, seq_me),
+            send_sem=wsend.at[i, r],
+            recv_sem=wrecv.at[i, r],
+            device_id=(same_core(r), exp_me),
+            device_id_type=MESH,
+        )
+
+    def relay(i, r):
+        shard, full = pairs[i]
+        origin = lax.rem(chip + chips - r, chips) * 2 + core
+        return pltpu.make_async_remote_copy(
+            src_ref=slot(full, shard, origin),
+            dst_ref=slot(full, shard, origin),
+            send_sem=psend.at[i, r],
+            recv_sem=precv.at[i, r],
+            device_id=(partner, exp_me),
+            device_id_type=MESH,
+        )
+
+    def hand_over(i):
+        shard, full = pairs[i]
+        return pltpu.make_async_remote_copy(
+            src_ref=shard,
+            dst_ref=slot(full, shard, seq_me),
+            send_sem=psend.at[i, 0],
+            recv_sem=precv.at[i, 0],
+            device_id=(partner, exp_me),
+            device_id_type=MESH,
+        )
+
+    def keep(i):
+        shard, full = pairs[i]
+        return pltpu.make_async_copy(shard, slot(full, shard, seq_me), own_sem.at[i])
+
+    @pl.loop(1, exp_size)
+    def _(r):
+        block(r).start()
+
+    @pl.loop(1, chips)
+    def _(r):
+        for i in range(3):
+            spread(i, r).start()
+
+    for i in range(3):
+        hand_over(i).start()
+        keep(i).start()
+    own.start()
+
+    @pl.loop(1, chips)
+    def _(r):
+        for i in range(3):
+            spread(i, r).wait_recv()
+            relay(i, r).start()
+
+    for i in range(3):
+        keep(i).wait()
+        hand_over(i).wait()
+
+    @pl.loop(1, chips)
+    def _(r):
+        for i in range(3):
+            spread(i, r).wait_send()
+            relay(i, r).wait()
+
+    own.wait()
+
+    @pl.loop(1, exp_size)
+    def _(r):
+        block(r).wait()
+
+
+def dispatch(rows, wg, wu, wd):
+    exp_size, seq_size = lax.axis_size("exp"), lax.axis_size("seq")
+    chips = seq_size // 2
+    hbm = pl.BlockSpec(memory_space=pl.ANY)
+
+    def full(shard):
+        return jax.ShapeDtypeStruct((shard.shape[0] * seq_size, shard.shape[1]), shard.dtype)
+
+    return pl.pallas_call(
+        dispatch_kernel,
+        out_shape=(jax.ShapeDtypeStruct(rows.shape, rows.dtype), full(wg), full(wu), full(wd)),
+        in_specs=[hbm] * 4,
+        out_specs=(hbm,) * 4,
+        scratch_shapes=[
+            pltpu.SemaphoreType.DMA((exp_size,)),
+            pltpu.SemaphoreType.DMA((exp_size,)),
+            pltpu.SemaphoreType.DMA((3,)),
+        ]
+        + [pltpu.SemaphoreType.DMA((3, chips))] * 4,
+        compiler_params=pltpu.CompilerParams(collective_id=0, has_side_effects=True),
+        name="dispatch",
+    )(rows, wg, wu, wd)
+
+
+def return_kernel(
+    rows_ref, q_ref, k_ref, v_ref, inv_ref, landed_ref, full_q, full_k, full_v, full_inv,
+    send_sem, recv_sem, own_sem, hsend, hrecv,
+):
+    exp_size, seq_size = lax.axis_size("exp"), lax.axis_size("seq")
+    exp_me, seq_me = lax.axis_index("exp"), lax.axis_index("seq")
+    greet(exp_size - 1, ((1, seq_size - 1, lambda r: lax.rem(seq_me + r, seq_size)),))
+    block, own = along_exp(rows_ref, landed_ref, send_sem, recv_sem)
+    pairs = ((q_ref, full_q, 2), (k_ref, full_k, 2), (v_ref, full_v, 1), (inv_ref, full_inv, 2))
+
+    def ends(i, other):
+        source, full, share = pairs[i]
+        depth, width = source.shape[0], full.shape[1]
+        return (
+            source.at[:, pl.ds(pl.multiple_of((other // share) * width, width), width)],
+            full.at[pl.ds(pl.multiple_of(seq_me * depth, depth), depth)],
+        )
+
+    def head(i, r):
+        other = lax.rem(seq_me + r, seq_size)
+        source, full = ends(i, other)
+        return pltpu.make_async_remote_copy(
+            src_ref=source,
+            dst_ref=full,
+            send_sem=hsend.at[i, r],
+            recv_sem=hrecv.at[i, r],
+            device_id=(other, exp_me),
+            device_id_type=MESH,
+        )
+
+    def keep(i):
+        source, full = ends(i, seq_me)
+        return pltpu.make_async_copy(source, full, own_sem.at[i])
+
+    @pl.loop(1, exp_size)
+    def _(r):
+        block(r).start()
+
+    @pl.loop(1, seq_size)
+    def _(r):
+        for i in range(4):
+            head(i, r).start()
+
+    for i in range(4):
+        keep(i).start()
+    own.start()
+    for i in range(4):
+        keep(i).wait()
+    own.wait()
+
+    @pl.loop(1, seq_size)
+    def _(r):
+        for i in range(4):
+            head(i, r).wait()
+
+    @pl.loop(1, exp_size)
+    def _(r):
+        block(r).wait()
+
+
+def give_back(rows, queries, key_rows, values, inverse, width):
+    exp_size, seq_size = lax.axis_size("exp"), lax.axis_size("seq")
+    hbm = pl.BlockSpec(memory_space=pl.ANY)
+    landed = jax.ShapeDtypeStruct((seq_size * queries.shape[0], width), queries.dtype)
+    return pl.pallas_call(
+        return_kernel,
+        out_shape=(jax.ShapeDtypeStruct(rows.shape, rows.dtype),) + (landed,) * 4,
+        in_specs=[hbm] * 5,
+        out_specs=(hbm,) * 5,
+        scratch_shapes=[
+            pltpu.SemaphoreType.DMA((exp_size,)),
+            pltpu.SemaphoreType.DMA((exp_size,)),
+            pltpu.SemaphoreType.DMA((4,)),
+            pltpu.SemaphoreType.DMA((4, seq_size)),
+            pltpu.SemaphoreType.DMA((4, seq_size)),
+        ],
+        compiler_params=pltpu.CompilerParams(collective_id=1, has_side_effects=True),
+        name="give_back",
+    )(rows, queries, key_rows, values, inverse)
 
 
 def per_device(
@@ -144,22 +389,19 @@
     source_row = jnp.full((experts * capacity,), tok_rows, jnp.int32).at[target].set(route_token)
     padded = jnp.concatenate([tokens, jnp.zeros((1, model_width), tokens.dtype)], axis=0)
     outgoing = jnp.take(padded, source_row, axis=0).reshape(experts, capacity, model_width)
-    incoming = lax.all_to_all(outgoing, "exp", split_axis=0, concat_axis=0, tiled=True)
+    incoming, full_gate, full_up, full_down = dispatch(outgoing, w_gate[0], w_up[0], w_down[0])
     expert_rows = incoming.reshape(-1, model_width)
-
-    def add_rows(portion):
-        return jnp.dot(expert_rows, portion, preferred_element_type=jnp.float32)
-
-    gate_proj_h = add_rows(lax.all_gather(w_gate[0], "seq", axis=0, tiled=True))
-    up_proj_h = add_rows(lax.all_gather(w_up[0], "seq", axis=0, tiled=True))
+    gate_proj_h = jnp.dot(expert_rows, full_gate, preferred_element_type=jnp.float32)
+    up_proj_h = jnp.dot(expert_rows, full_up, preferred_element_type=jnp.float32)
     hidden = (jax.nn.silu(gate_proj_h) * up_proj_h).astype(jnp.bfloat16)
-    produced = jnp.dot(
-        hidden,
-        lax.all_gather(w_down[0], "seq", axis=0, tiled=True),
-        preferred_element_type=jnp.float32,
-    )
+    produced = jnp.dot(hidden, full_down, preferred_element_type=jnp.float32)
     produced = produced.astype(jnp.bfloat16).reshape(exp_size, -1, model_width)
-    returned = lax.all_to_all(produced, "exp", split_axis=0, concat_axis=0, tiled=True)
+    heads_v = head_decay.shape[0]
+    heads_dev = heads_v // seq_size
+    key_dim = 2 * query_in.shape[2] // heads_v
+    returned, full_q, full_k, got_v, got_inv = give_back(
+        produced, query_in[0], key_in[0], value_in[0], block_inverse[0], key_dim
+    )
     back_rows = jnp.take(returned.reshape(-1, model_width), target, axis=0).reshape(
         tok_rows, routes_tok, model_width
     )
@@ -180,36 +422,14 @@
     routed = mixed.astype(jnp.bfloat16)
     residual = (tokens.astype(jnp.float32) + routed.astype(jnp.float32)).astype(jnp.bfloat16)
     logits = jnp.dot(residual, gate_proj, preferred_element_type=jnp.float32).astype(jnp.bfloat16)
-    heads_v = head_decay.shape[0]
-    heads_k = heads_v // 2
-    key_dim = query_in.shape[2] // heads_k
-    heads_dev = heads_v // seq_size
-    beta_logit = logits[:, :heads_v]
-    decay_logit = logits[:, heads_v:]
-    queries = query_in[0]
-    key_rows = key_in[0]
-    values_in = value_in[0]
-    inverse_in = block_inverse[0]
-
-    def repeated(values):
-        return jnp.repeat(values.reshape(tok_rows, heads_k, key_dim), 2, axis=1).reshape(
-            tok_rows, -1
-        )
-
-    full_q, full_k, got_v, got_inv, got_beta, got_decay = (
-        lax.all_to_all(repeated(queries), "seq", split_axis=1, concat_axis=0, tiled=True),
-        lax.all_to_all(repeated(key_rows), "seq", split_axis=1, concat_axis=0, tiled=True),
-        lax.all_to_all(values_in, "seq", split_axis=1, concat_axis=0, tiled=True),
-        lax.all_to_all(inverse_in, "seq", split_axis=1, concat_axis=0, tiled=True),
-        lax.all_to_all(beta_logit, "seq", split_axis=1, concat_axis=0, tiled=True),
-        lax.all_to_all(decay_logit, "seq", split_axis=1, concat_axis=0, tiled=True),
-    )
     seq_len = full_q.shape[0]
-    block_size = inverse_in.shape[1] // heads_v
+    block_size = block_inverse.shape[2] // heads_v
     block_count = seq_len // block_size
+    leaving = logits.T.reshape(2, seq_size, tok_rows).transpose(1, 0, 2)
+    gates = lax.all_to_all(leaving, "seq", split_axis=0, concat_axis=0, tiled=True)
+    gates = gates.transpose(1, 0, 2).reshape(2, block_count, block_size)
     head_start = lax.axis_index("seq") * heads_dev
     rate = lax.dynamic_slice_in_dim(head_decay, head_start, heads_dev).reshape(1, 1)
-    gates = jnp.stack([got_beta, got_decay]).reshape(2, block_count, block_size)
     flat_out = delta_rule(full_q, full_k, got_v, got_inv, gates, rate)
     core_out = lax.all_to_all(flat_out, "seq", split_axis=0, concat_axis=1, tiled=True)
     return (routed[None], core_out[None])

time: 440 us -> 311 us (0.71)
  waiting for transfers between devices: 271 us -> 6.24 us
  Pallas kernels: 29.4 us -> 240 us
  starting transfers between devices: 61.2 us -> 6.96 us
  between operations: 14.2 us -> 0.91 us
  local copies, waits for them, and re-layouts: 23.4 us -> 15.9 us
    all_to_all x8 -> x1, waiting for transfers between devices: 220 us -> 6.24 us  [per_device(): lax.all_to_all(leaving, 'seq', split_axis=0, concat_axis=0, tiled=True)]
    pallas_call x0 -> x2, Pallas kernels: none -> 211 us  [the longest x1 111 us: dispatch(): pl.pallas_call(dispatch_kernel, out_shape=(jax.ShapeDtypeStruct(rows.shap...]
    all_to_all x8 -> x1, starting transfers between devices: 61.1 us -> 6.96 us  [per_device(): lax.all_to_all(leaving, 'seq', split_axis=0, concat_axis=0, tiled=True)]
    all_gather x3 -> x0, waiting for transfers between devices: 48.8 us -> none  [the longest x1 48.8 us: per_device(): up_proj_h = add_rows(lax.all_gather(w_up[0], 'seq', axis=0, tiled=True))]
    unnamed x35 -> x19, local copies, waits for them, and re-layouts: 6.67 us -> 0.89 us
  transfers between devices with their start and end apart: 11 -> 1, of which waited for: 8 -> 1; matrix products, arithmetic and copies ran while one was open for 8% -> 0% of each run, Pallas kernels for 0% -> 0%
where the time goes in v2:
time: 311 us; the launch traced here: 309 us
  Pallas kernels  240 us (77%)
  blocking collectives  21.2 us (7%)
  local copies, waits for them, and re-layouts  15.9 us (5%)
  matrix products  10.2 us (3%)
  other arithmetic  7.32 us (2%)
  starting transfers between devices  6.96 us (2%)
  waiting for transfers between devices  6.24 us (2%)
    pallas_call x1, Pallas kernels, dispatch(): pl.pallas_call(dispatch_kernel, out_shape=(jax.ShapeDtypeStruct(rows.shap...  111 us
    pallas_call x1, Pallas kernels, give_back(): pl.pallas_call(return_kernel, out_shape=(jax.ShapeDtypeStruct(rows.shape,...  99.5 us
    pallas_call x1, Pallas kernels, delta_rule(): pl.pallas_call(functools.partial(delta_kernel, block_size), grid=(seq_len...  29.7 us
    all_to_all x1, blocking collectives, per_device(): lax.all_to_all(flat_out, 'seq', split_axis=0, concat_axis=1, tiled=True)  21.2 us
    all_to_all x1, starting transfers between devices, per_device(): lax.all_to_all(leaving, 'seq', split_axis=0, concat_axis=0, tiled=True)  6.96 us
    all_to_all x1, waiting for transfers between devices, per_device(): lax.all_to_all(leaving, 'seq', split_axis=0, concat_axis=0, tiled=True)  6.24 us
  transfers between devices with their start and end apart: 1, of which 1 were waited for; matrix products, arithmetic and copies ran while one was open for 0% of the time, Pallas kernels for 0%

profile of v2, /device:TPU:1, one launch (start us, length us, event | category | flops | bytes accessed | tf_op | source)
XLA Modules:
  0.0 309.2 jit_solution(7479669490819532436)
XLA Ops:
  0.6 0.0 copy-start
  0.6 0.8 copy.50
  1.5 0.1 eq.74
  1.6 0.1 reshape_squeeze.3
  1.8 0.7 broadcast_multiply_fusion
  2.5 0.6 reduce-window.6
  3.0 0.2 slice_reduce_fusion
  3.3 0.1 copy.55
  3.4 0.1 mul.65
  3.5 0.1 fusion.8
  3.6 1.4 scatter_custom_fusion
  5.1 0.1 reduce_sum.33
  5.2 0.1 broadcast_in_dim.41
  5.3 1.1 concatenate.3
  6.4 2.5 gather_fusion
  8.9 1.6 broadcast_select_fusion.rows_ref
  10.5 111.2 %dispatch.1 = (bf16[16,32,2048]{2,1,0:T(8,128)(2,1)}, bf16[2048,512]{1,0:T(8,128)(2,1)}, bf16[2048,512]{1,0:T(8,128)(2,1)}, bf16[512,2048]{1,0:T(8,128)(2,1)}) custom-call(bf16[16,32,2048]{2,1,0:T(8,128)(2,1)} %broadcast_select_fusion.rows_ref, bf16[64,512]{1,0:T(8,128)(2,1)} %bitcast.73, bf16[64,512]{1,0:T(8,128)(2,1)} %bitcast.74, bf16[16,2048]{1,0:T(8,128)(2,1)} %bitcast.75), custom_call_target="tpu_custom_call" | custom-call | tf_op jit(solution)/shard_map/dispatch/pallas_call | solution.py:262
  121.7 0.0 copy-start.6
  121.7 3.6 %fusion.14 = f32[512,512]{1,0:T(8,128)S(1)} fusion(bf16[512,2048]{1,0:T(8,128)(2,1)} %bitcast.82, bf16[2048,512]{1,0:T(8,128)(2,1)} %get-tuple-element.12), kind=kOutput, calls=%fused_computation.48 | convolution fusion | flops 1073741824 | bytes 5242880 | tf_op jit(solution)/shard_map/dot_general | solution.py:394
  125.3 0.0 copy-done.6
  125.3 6.1 %convolution_convert_fusion = bf16[512,2048]{1,0:T(8,128)(2,1)} fusion(bf16[512,2048]{1,0:T(8,128)(2,1)} %get-tuple-element.14, bf16[512,2048]{1,0:T(8,128)(2,1)S(1)} %bitcast.83, bf16[2048,512]{1,0:T(8,128)(2,1)} %get-tuple-element.13, f32[512,512]{1,0:T(8,128)S(1)} %fusion.14), kind=kOutput, calls=%fused_computation.3 | convolution fusion | flops 2150105088 | bytes 9437184 | tf_op jit(solution)/shard_map/dot_general | solution.py:397
  131.4 99.5 %give_back.1 = (bf16[16,32,2048]{2,1,0:T(8,128)(2,1)}, bf16[4096,128]{1,0:T(8,128)(2,1)}, bf16[4096,128]{1,0:T(8,128)(2,1)}, bf16[4096,128]{1,0:T(8,128)(2,1)}, bf16[4096,128]{1,0:T(8,128)(2,1)}) custom-call(bf16[16,32,2048]{2,1,0:T(8,128)(2,1)} %bitcast.66, bf16[128,2048]{1,0:T(8,128)(2,1)} %bitcast.70, bf16[128,2048]{1,0:T(8,128)(2,1)} %bitcast.71, ...), custom_call_target="tpu_custom_call" | custom-call | tf_op jit(solution)/shard_map/give_back/pallas_call | solution.py:342
  230.9 4.2 %gather_fusion.1 = bf16[256,2048]{1,0:T(8,128)(2,1)S(1)} fusion(bf16[512,2048]{1,0:T(8,128)(2,1)} %bitcast.62, s32[1024]{0:T(1024)S(1)} %pad_clamp_fusion), kind=kCustom, calls=%fused_computation.1 | custom fusion | bytes 2098176 | tf_op jit(solution)/shard_map/jit(_take)/gather | solution.py:405
  235.1 0.0 copy-start.3
  235.1 0.0 copy-start.4
  235.1 0.0 copy-start.7
  235.1 0.0 copy-start.5
  235.1 0.0 copy-start.2
  235.2 0.7 gather.15
  235.9 0.0 copy-start.8
  235.9 0.1 copy.53
  236.0 0.0 copy-done.3
  236.0 0.1 copy.54
  236.1 0.1 fusion.5
  236.2 0.2 fusion.3
  236.5 0.1 copy.49
  236.6 4.1 %multiply_reduce_fusion = bf16[128,2048]{1,0:T(8,128)(2,1)S(1)} fusion(bf16[128,2,2048]{2,1,0:T(2,128)(2,1)S(1)} %gather.15, pred[128,2]{1,0:T(8,128)(4,1)S(1)} %copy.54, f32[128,2]{1,0:T(8,128)S(1)} %copy.49), kind=kLoop, calls=%fused_computation.4 | loop fusion | flops 1835008 | bytes 1574144 | tf_op jit(solution)/shard_map/reduce_sum | solution.py:421
  240.8 0.0 copy-start.1
  240.8 0.3 convolution_convert_fusion.1
  241.1 0.6 copy.62
  241.7 7.0 %all-to-all-start = ((bf16[32,2,128]{2,1,0:T(2,128)(2,1)}), bf16[32,2,128]{2,1,0:T(2,128)(2,1)S(1)}, u32[]{:S(2)}, u32[]{:S(2)}) async-start(bf16[32,2,128]{2,1,0:T(2,128)(2,1)} %bitcast.61), calls=%async_computation | async-start | bytes 32768 | tf_op jit(solution)/shard_map/all_to_all | solution.py:429
  248.7 0.6 dynamic_slice.3
  249.3 6.2 %all-to-all-done = bf16[32,2,128]{2,1,0:T(2,128)(2,1)S(1)} async-done(((bf16[32,2,128]{2,1,0:T(2,128)(2,1)}), bf16[32,2,128]{2,1,0:T(2,128)(2,1)S(1)}, u32[]{:S(2)}, u32[]{:S(2)}) %all-to-all-start) | async-done | bytes 16416 | tf_op jit(solution)/shard_map/all_to_all | solution.py:429
  255.5 0.7 reshape.130.gate_ref
  256.2 29.7 %delta_rule.1 = bf16[4096,128]{1,0:T(8,128)(2,1)} custom-call(bf16[4096,128]{1,0:T(8,128)(2,1)} %get-tuple-element.16.q_ref, bf16[4096,128]{1,0:T(8,128)(2,1)} %get-tuple-element.17.k_ref, bf16[4096,128]{1,0:T(8,128)(2,1)} %get-tuple-element.18.v_ref, bf16[4096,128]{1,0:T(8,128)(2,1)} %get-tuple-element.19.inv_ref, bf16[2,64,64]{2,1,0:T(8,128)(2,1)} %reshape.130.gate_ref, ...), custom_call_target="tpu_custom_call" | custom-call | tf_op jit(solution)/shard_map/delta_rule/pallas_call | solution.py:94
  286.0 21.2 %all_to_all.21 = bf16[32,128,128]{2,1,0:T(8,128)(2,1)S(1)} all-to-all(bf16[32,128,128]{2,1,0:T(8,128)(2,1)} %bitcast.65), channel_id=1, replica_groups=mesh['seq'=32,'exp'=16] {'seq'}, dimensions={0} | all-to-all | bytes 2097152 | tf_op jit(solution)/shard_map/all_to_all | solution.py:434
  307.2 0.7 copy.58
  307.9 1.3 broadcast_in_dim.46
  (20 shorter events, 0.2 us)
Async XLA Ops:
  0.6 240.1 %copy-start = (bf16[2048,64]{0,1:T(8,128)(2,1)S(1)}, bf16[2048,64]{0,1:T(8,128)(2,1)}, u32[]{:S(2)}) copy-start(bf16[2048,64]{0,1:T(8,128)(2,1)} %param.22) | copy-start | bytes 786436
  121.7 3.6 %copy-start.6 = (bf16[16,32,2048]{2,1,0:T(8,128)(2,1)S(1)}, bf16[16,32,2048]{2,1,0:T(8,128)(2,1)}, u32[]{:S(2)}) copy-start(bf16[16,32,2048]{2,1,0:T(8,128)(2,1)} %get-tuple-element.11) | copy-start | bytes 6291460
  235.1 0.9 copy-start.3
  235.1 1.0 copy-start.4
  235.1 1.1 copy-start.7
  235.1 1.3 copy-start.5
  235.1 5.6 %copy-start.2 = (bf16[1,128,2048]{2,1,0:T(8,128)(2,1)S(1)}, bf16[1,128,2048]{2,1,0:T(8,128)(2,1)}, u32[]{:S(2)}) copy-start(bf16[1,128,2048]{2,1,0:T(8,128)(2,1)} %param.14) | copy-start | bytes 1572868
  235.9 12.8 %copy-start.8 = (f32[32]{0:T(128)S(1)}, f32[32]{0:T(128)}, u32[]{:S(2)}) copy-start(f32[32]{0:T(128)} %param.23) | copy-start | bytes 388
  240.8 45.2 %copy-start.1 = (bf16[128,2048]{1,0:T(8,128)(2,1)}, bf16[128,2048]{1,0:T(8,128)(2,1)S(1)}, u32[]{:S(2)}) copy-start(bf16[128,2048]{1,0:T(8,128)(2,1)S(1)} %multiply_reduce_fusion) | copy-start | bytes 1572868
  241.7 13.8 %all-to-all-start = ((bf16[32,2,128]{2,1,0:T(2,128)(2,1)}), bf16[32,2,128]{2,1,0:T(2,128)(2,1)S(1)}, u32[]{:S(2)}, u32[]{:S(2)}) async-start(bf16[32,2,128]{2,1,0:T(2,128)(2,1)} %bitcast.61), calls=%async_computation | async-start | bytes 32768 | tf_op jit(solution)/shard_map/all_to_all | solution.py:429

commit v3 on v2

--- a/solution.py
+++ b/solution.py
@@ -136,51 +136,99 @@
     pl.semaphore_wait(barrier, exp_peers + sum(count for _, count, _ in seq_peers))
 
 
-def along_exp(rows_ref, landed_ref, send_sem, recv_sem):
+def plane(number):
+    exp_size, reach = lax.axis_size("exp"), lax.axis_size("exp") // 2
+    return lax.rem(
+        lax.axis_index("exp") + exp_size + lax.rem(number, reach) - reach // 2, exp_size
+    )
+
+
+def plane_back(number):
+    exp_size, reach = lax.axis_size("exp"), lax.axis_size("exp") // 2
+    return lax.rem(
+        lax.axis_index("exp") + exp_size - lax.rem(number, reach) + reach // 2, exp_size
+    )
+
+
+def along_exp(rows_ref, landed_ref, send_sem, recv_sem, own_sem, where):
     exp_size = lax.axis_size("exp")
+    reach = exp_size // 2
     exp_me, seq_me = lax.axis_index("exp"), lax.axis_index("seq")
 
-    def block(r):
-        other = lax.rem(exp_me + r, exp_size)
-        return pltpu.make_async_remote_copy(
-            src_ref=rows_ref.at[other],
-            dst_ref=landed_ref.at[exp_me],
-            send_sem=send_sem.at[r],
-            recv_sem=recv_sem.at[r],
-            device_id=(seq_me, other),
-            device_id_type=MESH,
-        )
-
-    own = pltpu.make_async_copy(rows_ref.at[exp_me], landed_ref.at[exp_me], send_sem.at[0])
-    return block, own
+    def block(j):
+        return pltpu.make_async_remote_copy(
+            src_ref=rows_ref.at[j],
+            dst_ref=landed_ref.at[j],
+            send_sem=send_sem.at[j],
+            recv_sem=recv_sem.at[j],
+            device_id=(seq_me, where(j)),
+            device_id_type=MESH,
+        )
+
+    def own(n):
+        j = reach // 2 + n * reach
+        return pltpu.make_async_copy(rows_ref.at[j], landed_ref.at[j], own_sem.at[n])
+
+    def each(act, low, high):
+        @pl.loop(low, high)
+        def _(j):
+            act(block(j))
+            act(block(j + reach))
+
+    def lower(act):
+        each(act, 0, reach // 2)
+
+    def upper(act):
+        each(act, reach // 2 + 1, reach)
+
+    return lower, upper, own
 
 
 def dispatch_kernel(
-    rows_ref, wg_ref, wu_ref, wd_ref, landed_ref, full_g, full_u, full_d,
-    send_sem, recv_sem, own_sem, wsend, wrecv, psend, precv,
+    rows_ref, wg_ref, wu_ref, wd_ref,
+    landed_ref, full_g, full_u, full_d, mid_g, mid_u, mid_d, far_g, far_u, far_d,
+    send_sem, recv_sem, own_sem, keep_sem, csend, crecv, wsend, wrecv, psend, precv,
 ):
     exp_size, seq_size = lax.axis_size("exp"), lax.axis_size("seq")
     exp_me, seq_me = lax.axis_index("exp"), lax.axis_index("seq")
     chips = seq_size // 2
     chip, core = seq_me // 2, lax.rem(seq_me, 2)
     partner = chip * 2 + 1 - core
+    quarter = lax.rem(exp_me + exp_size // 4, exp_size)
 
     def same_core(r):
         return lax.rem(chip + r, chips) * 2 + core
 
     greet(exp_size - 1, ((1, chips - 1, same_core), (0, 1, lambda r: partner)))
-    block, own = along_exp(rows_ref, landed_ref, send_sem, recv_sem)
-    pairs = ((wg_ref, full_g), (wu_ref, full_u), (wd_ref, full_d))
-
-    def slot(full, shard, who):
+    lower, upper, own = along_exp(rows_ref, landed_ref, send_sem, recv_sem, own_sem, plane)
+    pairs = (
+        (wg_ref, full_g, 0), (wu_ref, full_u, 0), (wd_ref, full_d, 0),
+        (far_g, full_g, 1), (far_u, full_u, 1), (far_d, full_d, 1),
+    )
+    legs = (
+        (wg_ref, mid_g), (wu_ref, mid_u), (wd_ref, mid_d),
+        (mid_g, far_g), (mid_u, far_u), (mid_d, far_d),
+    )
+
+    def cross(i):
+        return pltpu.make_async_remote_copy(
+            src_ref=legs[i][0],
+            dst_ref=legs[i][1],
+            send_sem=csend.at[i],
+            recv_sem=crecv.at[i],
+            device_id=(seq_me, quarter),
+            device_id_type=MESH,
+        )
+
+    def slot(i, who):
+        shard, full, which = pairs[i]
         depth = shard.shape[0]
-        return full.at[pl.ds(pl.multiple_of(who * depth, depth), depth)]
+        return full.at[which, pl.ds(pl.multiple_of(who * depth, depth), depth)]
 
     def spread(i, r):
-        shard, full = pairs[i]
-        return pltpu.make_async_remote_copy(
-            src_ref=shard,
-            dst_ref=slot(full, shard, seq_me),
+        return pltpu.make_async_remote_copy(
+            src_ref=pairs[i][0],
+            dst_ref=slot(i, seq_me),
             send_sem=wsend.at[i, r],
             recv_sem=wrecv.at[i, r],
             device_id=(same_core(r), exp_me),
@@ -188,11 +236,10 @@
         )
 
     def relay(i, r):
-        shard, full = pairs[i]
         origin = lax.rem(chip + chips - r, chips) * 2 + core
         return pltpu.make_async_remote_copy(
-            src_ref=slot(full, shard, origin),
-            dst_ref=slot(full, shard, origin),
+            src_ref=slot(i, origin),
+            dst_ref=slot(i, origin),
             send_sem=psend.at[i, r],
             recv_sem=precv.at[i, r],
             device_id=(partner, exp_me),
@@ -200,10 +247,9 @@
         )
 
     def hand_over(i):
-        shard, full = pairs[i]
-        return pltpu.make_async_remote_copy(
-            src_ref=shard,
-            dst_ref=slot(full, shard, seq_me),
+        return pltpu.make_async_remote_copy(
+            src_ref=pairs[i][0],
+            dst_ref=slot(i, seq_me),
             send_sem=psend.at[i, 0],
             recv_sem=precv.at[i, 0],
             device_id=(partner, exp_me),
@@ -211,44 +257,55 @@
         )
 
     def keep(i):
-        shard, full = pairs[i]
-        return pltpu.make_async_copy(shard, slot(full, shard, seq_me), own_sem.at[i])
-
-    @pl.loop(1, exp_size)
-    def _(r):
-        block(r).start()
-
-    @pl.loop(1, chips)
-    def _(r):
-        for i in range(3):
-            spread(i, r).start()
+        return pltpu.make_async_copy(pairs[i][0], slot(i, seq_me), keep_sem.at[i])
+
+    def send_out(first):
+        @pl.loop(1, chips)
+        def _(r):
+            for i in range(first, first + 3):
+                spread(i, r).start()
+
+        for i in range(first, first + 3):
+            hand_over(i).start()
+            keep(i).start()
 
     for i in range(3):
-        hand_over(i).start()
-        keep(i).start()
-    own.start()
-
-    @pl.loop(1, chips)
-    def _(r):
-        for i in range(3):
-            spread(i, r).wait_recv()
-            relay(i, r).start()
-
+        cross(i).start()
+    send_out(0)
+    lower(lambda copy: copy.start())
+    own(0).start()
+    own(1).start()
     for i in range(3):
+        cross(i).wait_recv()
+        cross(i + 3).start()
+    for i in range(3):
+        cross(i + 3).wait_recv()
+    send_out(3)
+    upper(lambda copy: copy.start())
+
+    for first in (0, 3):
+
+        @pl.loop(1, chips)
+        def _(r):
+            for i in range(first, first + 3):
+                spread(i, r).wait_recv()
+                relay(i, r).start()
+
+    for i in range(6):
+        cross(i).wait_send()
         keep(i).wait()
         hand_over(i).wait()
 
     @pl.loop(1, chips)
     def _(r):
-        for i in range(3):
+        for i in range(6):
             spread(i, r).wait_send()
             relay(i, r).wait()
 
-    own.wait()
-
-    @pl.loop(1, exp_size)
-    def _(r):
-        block(r).wait()
+    own(0).wait()
+    own(1).wait()
+    lower(lambda copy: copy.wait())
+    upper(lambda copy: copy.wait())
 
 
 def dispatch(rows, wg, wu, wd):
@@ -257,86 +314,151 @@
     hbm = pl.BlockSpec(memory_space=pl.ANY)
 
     def full(shard):
-        return jax.ShapeDtypeStruct((shard.shape[0] * seq_size, shard.shape[1]), shard.dtype)
+        return jax.ShapeDtypeStruct((2, shard.shape[0] * seq_size, shard.shape[1]), shard.dtype)
+
+    def like(array):
+        return jax.ShapeDtypeStruct(array.shape, array.dtype)
 
     return pl.pallas_call(
         dispatch_kernel,
-        out_shape=(jax.ShapeDtypeStruct(rows.shape, rows.dtype), full(wg), full(wu), full(wd)),
+        out_shape=(like(rows), full(wg), full(wu), full(wd)) + (like(wg), like(wu), like(wd)) * 2,
         in_specs=[hbm] * 4,
-        out_specs=(hbm,) * 4,
+        out_specs=(hbm,) * 10,
         scratch_shapes=[
             pltpu.SemaphoreType.DMA((exp_size,)),
             pltpu.SemaphoreType.DMA((exp_size,)),
-            pltpu.SemaphoreType.DMA((3,)),
+            pltpu.SemaphoreType.DMA((2,)),
+            pltpu.SemaphoreType.DMA((6,)),
+            pltpu.SemaphoreType.DMA((6,)),
+            pltpu.SemaphoreType.DMA((6,)),
         ]
-        + [pltpu.SemaphoreType.DMA((3, chips))] * 4,
+        + [pltpu.SemaphoreType.DMA((6, chips))] * 4,
         compiler_params=pltpu.CompilerParams(collective_id=0, has_side_effects=True),
         name="dispatch",
-    )(rows, wg, wu, wd)
+    )(rows, wg, wu, wd)[:4]
 
 
 def return_kernel(
     rows_ref, q_ref, k_ref, v_ref, inv_ref, landed_ref, full_q, full_k, full_v, full_inv,
-    send_sem, recv_sem, own_sem, hsend, hrecv,
+    send_sem, recv_sem, own_sem, keep_sem, vsend, vrecv, hsend, hrecv, psend, precv,
 ):
     exp_size, seq_size = lax.axis_size("exp"), lax.axis_size("seq")
     exp_me, seq_me = lax.axis_index("exp"), lax.axis_index("seq")
+    chips = seq_size // 2
+    chip, core = seq_me // 2, lax.rem(seq_me, 2)
+    partner = chip * 2 + 1 - core
     greet(exp_size - 1, ((1, seq_size - 1, lambda r: lax.rem(seq_me + r, seq_size)),))
-    block, own = along_exp(rows_ref, landed_ref, send_sem, recv_sem)
-    pairs = ((q_ref, full_q, 2), (k_ref, full_k, 2), (v_ref, full_v, 1), (inv_ref, full_inv, 2))
-
-    def ends(i, other):
-        source, full, share = pairs[i]
-        depth, width = source.shape[0], full.shape[1]
-        return (
-            source.at[:, pl.ds(pl.multiple_of((other // share) * width, width), width)],
-            full.at[pl.ds(pl.multiple_of(seq_me * depth, depth), depth)],
-        )
+    lower, upper, own = along_exp(rows_ref, landed_ref, send_sem, recv_sem, own_sem, plane_back)
+    shared = ((q_ref, full_q), (k_ref, full_k), (inv_ref, full_inv))
+
+    def piece(source, full, number):
+        width = full.shape[1]
+        return source.at[:, pl.ds(pl.multiple_of(number * width, width), width)]
+
+    def slot(source, full, who):
+        depth = source.shape[0]
+        return full.at[pl.ds(pl.multiple_of(who * depth, depth), depth)]
 
     def head(i, r):
-        other = lax.rem(seq_me + r, seq_size)
-        source, full = ends(i, other)
-        return pltpu.make_async_remote_copy(
-            src_ref=source,
-            dst_ref=full,
+        other = lax.rem(chip + r, chips)
+        return pltpu.make_async_remote_copy(
+            src_ref=piece(*shared[i], other),
+            dst_ref=slot(*shared[i], seq_me),
             send_sem=hsend.at[i, r],
             recv_sem=hrecv.at[i, r],
+            device_id=(other * 2 + core, exp_me),
+            device_id_type=MESH,
+        )
+
+    def relay(i, r):
+        origin = lax.rem(chip + chips - r, chips) * 2 + core
+        return pltpu.make_async_remote_copy(
+            src_ref=slot(*shared[i], origin),
+            dst_ref=slot(*shared[i], origin),
+            send_sem=psend.at[i, r],
+            recv_sem=precv.at[i, r],
+            device_id=(partner, exp_me),
+            device_id_type=MESH,
+        )
+
+    def hand_over(i):
+        return pltpu.make_async_remote_copy(
+            src_ref=piece(*shared[i], chip),
+            dst_ref=slot(*shared[i], seq_me),
+            send_sem=psend.at[i, 0],
+            recv_sem=precv.at[i, 0],
+            device_id=(partner, exp_me),
+            device_id_type=MESH,
+        )
+
+    def keep(i):
+        return pltpu.make_async_copy(
+            piece(*shared[i], chip), slot(*shared[i], seq_me), keep_sem.at[i]
+        )
+
+    def value(r):
+        other = lax.rem(seq_me + r, seq_size)
+        return pltpu.make_async_remote_copy(
+            src_ref=piece(v_ref, full_v, other),
+            dst_ref=slot(v_ref, full_v, seq_me),
+            send_sem=vsend.at[r],
+            recv_sem=vrecv.at[r],
             device_id=(other, exp_me),
             device_id_type=MESH,
         )
 
-    def keep(i):
-        source, full = ends(i, seq_me)
-        return pltpu.make_async_copy(source, full, own_sem.at[i])
-
-    @pl.loop(1, exp_size)
-    def _(r):
-        block(r).start()
+    keep_v = pltpu.make_async_copy(
+        piece(v_ref, full_v, seq_me), slot(v_ref, full_v, seq_me), keep_sem.at[3]
+    )
+    lower(lambda copy: copy.start())
+    upper(lambda copy: copy.start())
+
+    @pl.loop(1, chips)
+    def _(r):
+        for i in range(3):
+            head(i, r).start()
 
     @pl.loop(1, seq_size)
     def _(r):
-        for i in range(4):
-            head(i, r).start()
-
-    for i in range(4):
+        value(r).start()
+
+    for i in range(3):
+        hand_over(i).start()
         keep(i).start()
-    own.start()
-    for i in range(4):
+    keep_v.start()
+    own(0).start()
+    own(1).start()
+
+    @pl.loop(1, chips)
+    def _(r):
+        for i in range(3):
+            head(i, r).wait_recv()
+            relay(i, r).start()
+
+    for i in range(3):
         keep(i).wait()
-    own.wait()
+        hand_over(i).wait()
+    keep_v.wait()
+    own(0).wait()
+    own(1).wait()
+
+    @pl.loop(1, chips)
+    def _(r):
+        for i in range(3):
+            head(i, r).wait_send()
+            relay(i, r).wait()
 
     @pl.loop(1, seq_size)
     def _(r):
-        for i in range(4):
-            head(i, r).wait()
-
-    @pl.loop(1, exp_size)
-    def _(r):
-        block(r).wait()
+        value(r).wait()
+
+    lower(lambda copy: copy.wait())
+    upper(lambda copy: copy.wait())
 
 
 def give_back(rows, queries, key_rows, values, inverse, width):
     exp_size, seq_size = lax.axis_size("exp"), lax.axis_size("seq")
+    chips = seq_size // 2
     hbm = pl.BlockSpec(memory_space=pl.ANY)
     landed = jax.ShapeDtypeStruct((seq_size * queries.shape[0], width), queries.dtype)
     return pl.pallas_call(
@@ -347,10 +469,12 @@
         scratch_shapes=[
             pltpu.SemaphoreType.DMA((exp_size,)),
             pltpu.SemaphoreType.DMA((exp_size,)),
+            pltpu.SemaphoreType.DMA((2,)),
             pltpu.SemaphoreType.DMA((4,)),
-            pltpu.SemaphoreType.DMA((4, seq_size)),
-            pltpu.SemaphoreType.DMA((4, seq_size)),
-        ],
+            pltpu.SemaphoreType.DMA((seq_size,)),
+            pltpu.SemaphoreType.DMA((seq_size,)),
+        ]
+        + [pltpu.SemaphoreType.DMA((3, chips))] * 4,
         compiler_params=pltpu.CompilerParams(collective_id=1, has_side_effects=True),
         name="give_back",
     )(rows, queries, key_rows, values, inverse)
@@ -384,18 +508,27 @@
     onehot = (flat_routes[:, None] == expert_range[None, :]).astype(jnp.int32)
     earlier = jnp.cumsum(onehot, axis=0) - onehot
     slot_index = jnp.sum(earlier * onehot, axis=1)
-    target = flat_routes * capacity + slot_index
+    turned = lax.rem(flat_routes - lax.axis_index("exp") + experts + experts // 4, experts)
+    target = turned * capacity + slot_index
     route_token = jnp.arange(tok_rows * routes_tok, dtype=jnp.int32) // routes_tok
     source_row = jnp.full((experts * capacity,), tok_rows, jnp.int32).at[target].set(route_token)
     padded = jnp.concatenate([tokens, jnp.zeros((1, model_width), tokens.dtype)], axis=0)
     outgoing = jnp.take(padded, source_row, axis=0).reshape(experts, capacity, model_width)
     incoming, full_gate, full_up, full_down = dispatch(outgoing, w_gate[0], w_up[0], w_down[0])
-    expert_rows = incoming.reshape(-1, model_width)
-    gate_proj_h = jnp.dot(expert_rows, full_gate, preferred_element_type=jnp.float32)
-    up_proj_h = jnp.dot(expert_rows, full_up, preferred_element_type=jnp.float32)
-    hidden = (jax.nn.silu(gate_proj_h) * up_proj_h).astype(jnp.bfloat16)
-    produced = jnp.dot(hidden, full_down, preferred_element_type=jnp.float32)
-    produced = produced.astype(jnp.bfloat16).reshape(exp_size, -1, model_width)
+    expert_rows = incoming.reshape(2, -1, model_width)
+    produced = []
+    for which in range(2):
+        gate_proj_h = jnp.dot(
+            expert_rows[which], full_gate[which], preferred_element_type=jnp.float32
+        )
+        up_proj_h = jnp.dot(expert_rows[which], full_up[which], preferred_element_type=jnp.float32)
+        hidden = (jax.nn.silu(gate_proj_h) * up_proj_h).astype(jnp.bfloat16)
+        produced.append(
+            jnp.dot(hidden, full_down[which], preferred_element_type=jnp.float32).astype(
+                jnp.bfloat16
+            )
+        )
+    produced = jnp.concatenate(produced, axis=0).reshape(exp_size, -1, model_width)
     heads_v = head_decay.shape[0]
     heads_dev = heads_v // seq_size
     key_dim = 2 * query_in.shape[2] // heads_v

time: 311 us -> 316 us (1.016)
  starting transfers between devices: 6.96 us -> 24.2 us
  Pallas kernels: 240 us -> 225 us
    pallas_call x1, Pallas kernels: 99.5 us -> 76.7 us  [give_back(): pl.pallas_call(return_kernel, out_shape=(jax.ShapeDtypeStruct(rows.shape,...]
    all_to_all x1, starting transfers between devices: 6.96 us -> 24.2 us  [per_device(): lax.all_to_all(leaving, 'seq', split_axis=0, concat_axis=0, tiled=True)]
    pallas_call x1, Pallas kernels: 111 us -> 118 us  [dispatch(): pl.pallas_call(dispatch_kernel, out_shape=(like(rows), full(wg), full(wu)...]
    dot_general x2 -> x4, matrix products: 9.67 us -> 10.6 us  [the longest x2 7.53 us: per_device(): jnp.dot(hidden, full_down[which], preferred_element_type=jnp.float32)]
where the time goes in v3:
time: 316 us
  Pallas kernels  225 us (71%)
  starting transfers between devices  24.2 us (8%)
  blocking collectives  21.2 us (7%)
  local copies, waits for them, and re-layouts  18.7 us (6%)
  matrix products  11.1 us (4%)
  other arithmetic  8.83 us (3%)
  waiting for transfers between devices  6.24 us (2%)
    pallas_call x1, Pallas kernels, dispatch(): pl.pallas_call(dispatch_kernel, out_shape=(like(rows), full(wg), full(wu)...  118 us
    pallas_call x1, Pallas kernels, give_back(): pl.pallas_call(return_kernel, out_shape=(jax.ShapeDtypeStruct(rows.shape,...  76.7 us
    pallas_call x1, Pallas kernels, delta_rule(): pl.pallas_call(functools.partial(delta_kernel, block_size), grid=(seq_len...  29.7 us
    all_to_all x1, starting transfers between devices, per_device(): lax.all_to_all(leaving, 'seq', split_axis=0, concat_axis=0, tiled=True)  24.2 us
    all_to_all x1, blocking collectives, per_device(): lax.all_to_all(flat_out, 'seq', split_axis=0, concat_axis=1, tiled=True)  21.2 us
    dot_general x2, matrix products, per_device(): jnp.dot(hidden, full_down[which], preferred_element_type=jnp.float32)  7.53 us
  transfers between devices with their start and end apart: 1, of which 1 were waited for; matrix products, arithmetic and copies ran while one was open for 0% of the time, Pallas kernels for 0%

profile of v3, /device:TPU:1, one launch (start us, length us, event | category | flops | bytes accessed | tf_op | source)
XLA Modules:
  0.0 315.9 jit_solution(15693307208187829856)
XLA Ops:
  0.6 0.0 copy-start
  0.6 0.8 copy.50
  1.5 0.1 eq.74
  1.6 0.1 reshape_squeeze.3
  1.8 0.6 reduce-window.6
  2.4 0.2 slice_reduce_fusion
  2.6 0.7 subtract_add_fusion
  3.3 0.1 copy.55
  3.4 0.1 add.96
  3.5 0.1 fusion.50
  3.6 1.4 scatter_custom_fusion
  5.1 0.1 reduce_sum.33
  5.2 0.1 broadcast_in_dim.41
  5.3 1.1 concatenate.6
  6.4 2.5 gather_fusion
  8.9 1.6 broadcast_select_fusion.rows_ref
  10.5 118.2 %dispatch.1 = (bf16[16,32,2048]{2,1,0:T(8,128)(2,1)}, bf16[2,2048,512]{2,1,0:T(8,128)(2,1)}, bf16[2,2048,512]{2,1,0:T(8,128)(2,1)}, bf16[2,512,2048]{2,1,0:T(8,1...) custom-call(bf16[16,32,2048]{2,1,0:T(8,128)(2,1)} %broadcast_select_, ...), custom_call_target="tpu_custom_call" | custom-call | tf_op jit(solution)/shard_map/dispatch/pallas_call | solution.py:322
  128.7 1.8 fusion.63
  130.5 1.0 copy-done.6
  131.5 1.5 fusion.8
  133.0 1.5 fusion.3
  134.6 3.8 %convolution_convert_fusion.1 = bf16[256,2048]{1,0:T(8,128)(2,1)S(1)} fusion(bf16[2,512,2048]{2,1,0:T(8,128)(2,1)} %get-tuple-element.14, bf16[256,2048]{1,0:T(8,128)(2,1)S(1)} %bitcast.103, bf16[2,2048,512]{2,1,0:T(8,128)(2,1)} %get-tuple-element.13, f32[256,512]{1,0:T(8,128)} %fusion.8), kind=kOutput, calls=%fused_computation.4 | convolution fusion | flops 1075052544 | bytes 6815744 | tf_op jit(solution)/shard_map/dot_general | solution.py:527
  138.3 3.8 %convolution_convert_fusion = bf16[256,2048]{1,0:T(8,128)(2,1)S(1)} fusion(bf16[2,512,2048]{2,1,0:T(8,128)(2,1)} %get-tuple-element.14, bf16[256,2048]{1,0:T(8,128)(2,1)S(1)} %bitcast.101, bf16[2,2048,512]{2,1,0:T(8,128)(2,1)} %get-tuple-element.13, f32[256,512]{1,0:T(8,128)} %fusion.3), kind=kOutput, calls=%fused_computation.3 | convolution fusion | flops 1075052544 | bytes 6815744 | tf_op jit(solution)/shard_map/dot_general | solution.py:527
  142.1 1.5 pad_maximum_fusion
  143.6 76.7 %give_back.1 = (bf16[16,32,2048]{2,1,0:T(8,128)(2,1)}, bf16[4096,128]{1,0:T(8,128)(2,1)}, bf16[4096,128]{1,0:T(8,128)(2,1)}, bf16[4096,128]{1,0:T(8,128)(2,1)}, bf16[4096,128]{1,0:T(8,128)(2,1)}) custom-call(bf16[16,32,2048]{2,1,0:T(8,128)(2,1)} %bitcast.94, bf16[128,2048]{1,0:T(8,128)(2,1)} %bitcast.104, bf16[128,2048]{1,0:T(8,128)(2,1)} %bitcast.105, ...), custom_call_target="tpu_custom_call" | custom-call | tf_op jit(solution)/shard_map/give_back/pallas_call | solution.py:464
  220.3 4.2 %gather_fusion.1 = bf16[256,2048]{1,0:T(8,128)(2,1)S(1)} fusion(bf16[512,2048]{1,0:T(8,128)(2,1)} %bitcast.92, s32[1024]{0:T(1024)S(1)} %pad_clamp_fusion), kind=kCustom, calls=%fused_computation.1 | custom fusion | bytes 2098176 | tf_op jit(solution)/shard_map/jit(_take)/gather | solution.py:538
  224.5 0.0 copy-start.3
  224.5 0.0 copy-start.4
  224.6 0.0 copy-start.7
  224.6 0.7 gather.15
  225.3 0.0 copy-start.8
  225.3 0.1 copy.53
  225.4 0.1 copy.54
  225.6 0.1 fusion.47
  225.7 0.2 fusion.45
  225.9 0.1 copy.49
  226.1 4.1 %multiply_reduce_fusion = bf16[128,2048]{1,0:T(8,128)(2,1)S(1)} fusion(bf16[128,2,2048]{2,1,0:T(2,128)(2,1)S(1)} %gather.15, pred[128,2]{1,0:T(8,128)(4,1)S(1)} %copy.54, f32[128,2]{1,0:T(8,128)S(1)} %copy.49), kind=kLoop, calls=%fused_computation.16 | loop fusion | flops 1835008 | bytes 1574144 | tf_op jit(solution)/shard_map/reduce_sum | solution.py:554
  230.2 0.0 copy-start.1
  230.2 0.3 convolution_convert_fusion.2
  230.5 0.6 copy.62
  231.1 24.2 %all-to-all-start = ((bf16[32,2,128]{2,1,0:T(2,128)(2,1)}), bf16[32,2,128]{2,1,0:T(2,128)(2,1)S(1)}, u32[]{:S(2)}, u32[]{:S(2)}) async-start(bf16[32,2,128]{2,1,0:T(2,128)(2,1)} %bitcast.91), calls=%async_computation | async-start | bytes 32768 | tf_op jit(solution)/shard_map/all_to_all | solution.py:562
  255.4 0.6 dynamic_slice.3
  256.0 6.2 %all-to-all-done = bf16[32,2,128]{2,1,0:T(2,128)(2,1)S(1)} async-done(((bf16[32,2,128]{2,1,0:T(2,128)(2,1)}), bf16[32,2,128]{2,1,0:T(2,128)(2,1)S(1)}, u32[]{:S(2)}, u32[]{:S(2)}) %all-to-all-start) | async-done | bytes 16416 | tf_op jit(solution)/shard_map/all_to_all | solution.py:562
  262.3 0.7 reshape.157.gate_ref
  262.9 29.7 %delta_rule.1 = bf16[4096,128]{1,0:T(8,128)(2,1)} custom-call(bf16[4096,128]{1,0:T(8,128)(2,1)} %get-tuple-element.16.q_ref, bf16[4096,128]{1,0:T(8,128)(2,1)} %get-tuple-element.17.k_ref, bf16[4096,128]{1,0:T(8,128)(2,1)} %get-tuple-element.18.v_ref, bf16[4096,128]{1,0:T(8,128)(2,1)} %get-tuple-element.19.inv_ref, bf16[2,64,64]{2,1,0:T(8,128)(2,1)} %reshape.157.gate_ref, ...), custom_call_target="tpu_custom_call" | custom-call | tf_op jit(solution)/shard_map/delta_rule/pallas_call | solution.py:94
  292.7 21.2 %all_to_all.21 = bf16[32,128,128]{2,1,0:T(8,128)(2,1)S(1)} all-to-all(bf16[32,128,128]{2,1,0:T(8,128)(2,1)} %bitcast.96), channel_id=1, replica_groups=mesh['seq'=32,'exp'=16] {'seq'}, dimensions={0} | all-to-all | bytes 2097152 | tf_op jit(solution)/shard_map/all_to_all | solution.py:567
  313.9 0.7 copy.58
  314.6 1.3 broadcast_in_dim.46
  (24 shorter events, 0.2 us)
Async XLA Ops:
  0.6 229.6 %copy-start = (bf16[2048,64]{0,1:T(8,128)(2,1)S(1)}, bf16[2048,64]{0,1:T(8,128)(2,1)}, u32[]{:S(2)}) copy-start(bf16[2048,64]{0,1:T(8,128)(2,1)} %param.22) | copy-start | bytes 786436
  128.7 2.8 copy-start.6
  224.5 0.9 copy-start.3
  224.5 1.0 copy-start.4
  224.6 1.1 copy-start.7
  224.6 1.4 copy-start.5
  224.6 5.6 %copy-start.2 = (bf16[1,128,2048]{2,1,0:T(8,128)(2,1)S(1)}, bf16[1,128,2048]{2,1,0:T(8,128)(2,1)}, u32[]{:S(2)}) copy-start(bf16[1,128,2048]{2,1,0:T(8,128)(2,1)} %param.14) | copy-start | bytes 1572868
  225.3 30.1 %copy-start.8 = (f32[32]{0:T(128)S(1)}, f32[32]{0:T(128)}, u32[]{:S(2)}) copy-start(f32[32]{0:T(128)} %param.23) | copy-start | bytes 388
  230.2 62.5 %copy-start.1 = (bf16[128,2048]{1,0:T(8,128)(2,1)}, bf16[128,2048]{1,0:T(8,128)(2,1)S(1)}, u32[]{:S(2)}) copy-start(bf16[128,2048]{1,0:T(8,128)(2,1)S(1)} %multiply_reduce_fusion) | copy-start | bytes 1572868
  231.1 31.1 %all-to-all-start = ((bf16[32,2,128]{2,1,0:T(2,128)(2,1)}), bf16[32,2,128]{2,1,0:T(2,128)(2,1)S(1)}, u32[]{:S(2)}, u32[]{:S(2)}) async-start(bf16[32,2,128]{2,1,0:T(2,128)(2,1)} %bitcast.91), calls=%async_computation | async-start | bytes 32768 | tf_op jit(solution)/shard_map/all_to_all | solution.py:562

commit v4 on v2

--- a/solution.py
+++ b/solution.py
@@ -10,7 +10,10 @@
 highest = lax.Precision.HIGHEST
 
 
-def delta_kernel(block_size, q_ref, k_ref, v_ref, inv_ref, gate_ref, rate_ref, out_ref, state_ref, beta_ref, cum_ref):
+def delta_kernel(
+    block_size, q_ref, k_ref, v_ref, inv_ref, gate_ref, rate_ref, out_ref,
+    state_ref, beta_ref, cum_ref, done_ref, gates_ref, gsend, grecv, osend, orecv,
+):
     step = pl.program_id(0)
     chunk_rows, key_dim = q_ref.shape
     per_chunk = chunk_rows // block_size
@@ -19,18 +22,99 @@
     diagonal = rows_i == cols_i
     below = rows_i > cols_i
     causal = rows_i >= cols_i
+    seq_size = lax.axis_size("seq")
+    exp_me, seq_me = lax.axis_index("exp"), lax.axis_index("seq")
+    tok_rows = out_ref.shape[0]
+    owners = chunk_rows // tok_rows
+
+    def gate_copy(r):
+        other = lax.rem(seq_me + r, seq_size)
+        return pltpu.make_async_remote_copy(
+            src_ref=gate_ref.at[other],
+            dst_ref=gates_ref.at[seq_me],
+            send_sem=gsend.at[r],
+            recv_sem=grecv.at[r],
+            device_id=(other, exp_me),
+            device_id_type=MESH,
+        )
+
+    def out_ends(owner):
+        return (
+            done_ref.at[pl.ds(pl.multiple_of(owner * tok_rows, tok_rows), tok_rows)],
+            out_ref.at[:, pl.ds(pl.multiple_of(seq_me * key_dim, key_dim), key_dim)],
+        )
+
+    def out_copy(r):
+        other = lax.rem(seq_me + r, seq_size)
+        source, landing = out_ends(other)
+        return pltpu.make_async_remote_copy(
+            src_ref=source,
+            dst_ref=landing,
+            send_sem=osend.at[r],
+            recv_sem=orecv.at[r],
+            device_id=(other, exp_me),
+            device_id_type=MESH,
+        )
+
+    def out_own():
+        source, landing = out_ends(seq_me)
+        return pltpu.make_async_copy(source, landing, osend.at[0])
+
+    def send_chunk(number):
+        for place in range(owners):
+            owner = number * owners + place
+
+            @pl.when(owner != seq_me)
+            def _():
+                out_copy(lax.rem(owner + seq_size - seq_me, seq_size)).start()
+
+            @pl.when(owner == seq_me)
+            def _():
+                out_own().start()
 
     @pl.when(step == 0)
     def _():
+        barrier = pltpu.get_barrier_semaphore()
+
+        @pl.loop(1, seq_size)
+        def _(r):
+            pl.semaphore_signal(
+                barrier,
+                inc=1,
+                device_id=(lax.rem(seq_me + r, seq_size), exp_me),
+                device_id_type=MESH,
+            )
+
+        pl.semaphore_wait(barrier, seq_size - 1)
+        own = pltpu.make_async_copy(gate_ref.at[seq_me], gates_ref.at[seq_me], gsend.at[0])
+        own.start()
+
+        @pl.loop(1, seq_size)
+        def _(r):
+            gate_copy(r).start()
+
         state_ref[...] = jnp.zeros_like(state_ref)
-        beta_ref[...] = jax.nn.sigmoid(gate_ref[0].astype(jnp.float32))
-        raw = gate_ref[1].astype(jnp.float32)
+        own.wait()
+
+        @pl.loop(1, seq_size)
+        def _(r):
+            gate_copy(r).wait()
+
+        beta_ref[...] = jax.nn.sigmoid(gates_ref[:, 0, :])
+        raw = gates_ref[:, 1, :]
         soft = jnp.maximum(raw, 0.0) + jnp.log1p(jnp.exp(-jnp.abs(raw)))
         log_decay = -jnp.exp(rate_ref[0, 0]) * soft
-        upper = (rows_i <= cols_i).astype(jnp.float32)
+        rows_t = lax.broadcasted_iota(jnp.int32, (tok_rows, tok_rows), 0)
+        cols_t = lax.broadcasted_iota(jnp.int32, (tok_rows, tok_rows), 1)
+        same = rows_t // block_size == cols_t // block_size
+        upper = jnp.where(same & (rows_t <= cols_t), 1.0, 0.0)
         cum_ref[...] = jnp.dot(
             log_decay, upper, precision=highest, preferred_element_type=jnp.float32
         )
+
+    @pl.when(step > 0)
+    def _():
+        send_chunk(step - 1)
 
     odd = lax.rem(lax.axis_index("seq"), 2) == 1
 
@@ -50,10 +134,12 @@
     state = state_ref[...]
     for piece in range(per_chunk):
         span = pl.ds(piece * block_size, block_size)
-        block = step * per_chunk + piece
-        cum_row = cum_ref[pl.ds(block, 1), :]
+        fold = tok_rows // block_size
+        line = pl.ds(step * owners + piece // fold, 1)
+        part = slice(piece % fold * block_size, (piece % fold + 1) * block_size)
+        cum_row = cum_ref[line, part]
         cum_col = column(cum_row)
-        beta_col = column(beta_ref[pl.ds(block, 1), :])
+        beta_col = column(beta_ref[line, part])
         last = cum_row[:, block_size - 1 :]
         grow = jnp.exp(cum_col)
         query_n = normal(q_ref[span, :], key_dim ** (-0.5))
@@ -74,19 +160,30 @@
         write = dot(new_base.astype(jnp.bfloat16), key_decay, (0, 0))
         held = state.astype(jnp.bfloat16)
         fresh = (new_base - dot(key_mix, held, (1, 1))).astype(jnp.bfloat16)
-        out_ref[span, :] = (dot(query_gate, held, (1, 1)) + dot(weights, fresh, (1, 0))).astype(
+        spot = pl.ds(pl.multiple_of(step * chunk_rows + piece * block_size, block_size), block_size)
+        done_ref[spot, :] = (dot(query_gate, held, (1, 1)) + dot(weights, fresh, (1, 0))).astype(
             jnp.bfloat16
         )
         state = jnp.exp(last) * state + (write - dot(held, erase, (1, 0)))
     state_ref[...] = state
+
+    @pl.when(step == pl.num_programs(0) - 1)
+    def _():
+        send_chunk(step)
+        out_own().wait()
+
+        @pl.loop(1, seq_size)
+        def _(r):
+            out_copy(r).wait()
 
 
 def delta_rule(queries, key_rows, values, inverse, gates, rate):
     seq_len, key_dim = queries.shape
     value_dim = values.shape[1]
     block_size = inverse.shape[1] // 2
-    block_count = seq_len // block_size
-    chunk = 8 * block_size
+    seq_size = lax.axis_size("seq")
+    tok_rows = seq_len // seq_size
+    chunk = 4 * tok_rows
 
     def rows(width):
         return pl.BlockSpec((chunk, width), lambda i: (i, 0))
@@ -94,21 +191,25 @@
     return pl.pallas_call(
         functools.partial(delta_kernel, block_size),
         grid=(seq_len // chunk,),
-        out_shape=jax.ShapeDtypeStruct((seq_len, value_dim), jnp.bfloat16),
+        out_shape=jax.ShapeDtypeStruct((tok_rows, seq_size * value_dim), jnp.bfloat16),
         in_specs=[
             rows(key_dim),
             rows(key_dim),
             rows(value_dim),
             rows(2 * block_size),
-            pl.BlockSpec((2, block_count, block_size), lambda i: (0, 0, 0)),
+            pl.BlockSpec(memory_space=pl.ANY),
             pl.BlockSpec((1, 1), lambda i: (0, 0), memory_space=pltpu.SMEM),
         ],
-        out_specs=rows(value_dim),
+        out_specs=pl.BlockSpec(memory_space=pl.ANY),
         scratch_shapes=[
             pltpu.VMEM((value_dim, key_dim), jnp.float32),
-            pltpu.VMEM((block_count, block_size), jnp.float32),
-            pltpu.VMEM((block_count, block_size), jnp.float32),
-        ],
+            pltpu.VMEM((seq_size, tok_rows), jnp.float32),
+            pltpu.VMEM((seq_size, tok_rows), jnp.float32),
+            pltpu.VMEM((seq_len, value_dim), jnp.bfloat16),
+            pltpu.VMEM(gates.shape, jnp.float32),
+        ]
+        + [pltpu.SemaphoreType.DMA((seq_size,))] * 4,
+        compiler_params=pltpu.CompilerParams(collective_id=2, has_side_effects=True),
         name="delta_rule",
     )(queries, key_rows, values, inverse, gates, rate)
 
@@ -422,16 +523,11 @@
     routed = mixed.astype(jnp.bfloat16)
     residual = (tokens.astype(jnp.float32) + routed.astype(jnp.float32)).astype(jnp.bfloat16)
     logits = jnp.dot(residual, gate_proj, preferred_element_type=jnp.float32).astype(jnp.bfloat16)
-    seq_len = full_q.shape[0]
-    block_size = block_inverse.shape[2] // heads_v
-    block_count = seq_len // block_size
-    leaving = logits.T.reshape(2, seq_size, tok_rows).transpose(1, 0, 2)
-    gates = lax.all_to_all(leaving, "seq", split_axis=0, concat_axis=0, tiled=True)
-    gates = gates.transpose(1, 0, 2).reshape(2, block_count, block_size)
+    leaving = logits.T.astype(jnp.float32).reshape(2, seq_size, tok_rows).transpose(1, 0, 2)
+    gates = jnp.pad(leaving, ((0, 0), (0, 6), (0, 0)))
     head_start = lax.axis_index("seq") * heads_dev
     rate = lax.dynamic_slice_in_dim(head_decay, head_start, heads_dev).reshape(1, 1)
-    flat_out = delta_rule(full_q, full_k, got_v, got_inv, gates, rate)
-    core_out = lax.all_to_all(flat_out, "seq", split_axis=0, concat_axis=1, tiled=True)
+    core_out = delta_rule(full_q, full_k, got_v, got_inv, gates, rate)
     return (routed[None], core_out[None])
 
 

time: 311 us -> 300 us (0.965)
  Pallas kernels: 240 us -> 262 us
  blocking collectives: 21.2 us -> 0 us
  starting transfers between devices: 6.96 us -> 0 us
  waiting for transfers between devices: 6.24 us -> 0 us
    pallas_call x1, Pallas kernels: 29.7 us -> 51.1 us  [delta_rule(): pl.pallas_call(functools.partial(delta_kernel, block_size), grid=(seq_len...]
    all_to_all x1 -> x0, blocking collectives: 21.2 us -> none  [per_device(): lax.all_to_all(flat_out, 'seq', split_axis=0, concat_axis=1, tiled=True)]
    all_to_all x1 -> x0, starting transfers between devices: 6.96 us -> none  [per_device(): lax.all_to_all(leaving, 'seq', split_axis=0, concat_axis=0, tiled=True)]
    all_to_all x1 -> x0, waiting for transfers between devices: 6.24 us -> none  [per_device(): lax.all_to_all(leaving, 'seq', split_axis=0, concat_axis=0, tiled=True)]
  transfers between devices with their start and end apart: 1 -> 0, of which waited for: 1 -> 0; matrix products, arithmetic and copies ran while one was open for 0% -> 0% of each run, Pallas kernels for 0% -> 0%
where the time goes in v4:
time: 300 us; the launch traced here: 296 us
  Pallas kernels  262 us (87%)
  local copies, waits for them, and re-layouts  15 us (5%)
  matrix products  10.2 us (3%)
  other arithmetic  8 us (3%)
    pallas_call x1, Pallas kernels, dispatch(): pl.pallas_call(dispatch_kernel, out_shape=(jax.ShapeDtypeStruct(rows.shap...  111 us
    pallas_call x1, Pallas kernels, give_back(): pl.pallas_call(return_kernel, out_shape=(jax.ShapeDtypeStruct(rows.shape,...  99.5 us
    pallas_call x1, Pallas kernels, delta_rule(): pl.pallas_call(functools.partial(delta_kernel, block_size), grid=(seq_len...  51.1 us
    dot_general x1, matrix products, per_device(): produced = jnp.dot(hidden, full_down, preferred_element_type=jnp.float32)  6.04 us

profile of v4, /device:TPU:1, one launch (start us, length us, event | category | flops | bytes accessed | tf_op | source)
XLA Modules:
  0.0 295.9 jit_solution(8689671469751151941)
XLA Ops:
  0.6 0.0 copy-start
  0.6 0.8 copy.37
  1.5 0.1 eq.74
  1.6 0.6 reduce-window.6
  2.2 0.2 slice_reduce_fusion
  2.4 0.1 reshape_squeeze.3
  2.6 0.1 fusion.8
  2.7 0.7 broadcast_multiply_fusion
  3.4 0.1 copy.42
  3.5 0.1 mul.65
  3.6 1.4 scatter_custom_fusion
  5.1 1.1 concatenate.3
  6.2 2.5 gather_fusion
  8.7 0.1 broadcast_in_dim.41
  8.7 1.6 broadcast_select_fusion.rows_ref
  10.4 111.2 %dispatch.1 = (bf16[16,32,2048]{2,1,0:T(8,128)(2,1)}, bf16[2048,512]{1,0:T(8,128)(2,1)}, bf16[2048,512]{1,0:T(8,128)(2,1)}, bf16[512,2048]{1,0:T(8,128)(2,1)}) custom-call(bf16[16,32,2048]{2,1,0:T(8,128)(2,1)} %broadcast_select_fusion.rows_ref, bf16[64,512]{1,0:T(8,128)(2,1)} %bitcast.70, bf16[64,512]{1,0:T(8,128)(2,1)} %bitcast.71, bf16[16,2048]{1,0:T(8,128)(2,1)} %bitcast.72), custom_call_target="tpu_custom_call" | custom-call | tf_op jit(solution)/shard_map/dispatch/pallas_call | solution.py:363
  121.6 0.0 copy-start.6
  121.6 3.6 %fusion.14 = f32[512,512]{1,0:T(8,128)S(1)} fusion(bf16[512,2048]{1,0:T(8,128)(2,1)} %bitcast.79, bf16[2048,512]{1,0:T(8,128)(2,1)} %get-tuple-element.12), kind=kOutput, calls=%fused_computation.49 | convolution fusion | flops 1073741824 | bytes 5242880 | tf_op jit(solution)/shard_map/dot_general | solution.py:495
  125.2 0.0 copy-done.6
  125.2 6.0 %convolution_convert_fusion = bf16[512,2048]{1,0:T(8,128)(2,1)} fusion(bf16[512,2048]{1,0:T(8,128)(2,1)} %get-tuple-element.14, bf16[512,2048]{1,0:T(8,128)(2,1)S(1)} %bitcast.80, bf16[2048,512]{1,0:T(8,128)(2,1)} %get-tuple-element.13, f32[512,512]{1,0:T(8,128)S(1)} %fusion.14), kind=kOutput, calls=%fused_computation.3 | convolution fusion | flops 2150105088 | bytes 9437184 | tf_op jit(solution)/shard_map/dot_general | solution.py:498
  131.2 99.5 %give_back.1 = (bf16[16,32,2048]{2,1,0:T(8,128)(2,1)}, bf16[4096,128]{1,0:T(8,128)(2,1)}, bf16[4096,128]{1,0:T(8,128)(2,1)}, bf16[4096,128]{1,0:T(8,128)(2,1)}, bf16[4096,128]{1,0:T(8,128)(2,1)}) custom-call(bf16[16,32,2048]{2,1,0:T(8,128)(2,1)} %bitcast.63, bf16[128,2048]{1,0:T(8,128)(2,1)} %bitcast.67, bf16[128,2048]{1,0:T(8,128)(2,1)} %bitcast.68, ...), custom_call_target="tpu_custom_call" | custom-call | tf_op jit(solution)/shard_map/give_back/pallas_call | solution.py:443
  230.8 4.2 %gather_fusion.1 = bf16[256,2048]{1,0:T(8,128)(2,1)S(1)} fusion(bf16[512,2048]{1,0:T(8,128)(2,1)} %bitcast.60, s32[1024]{0:T(1024)S(1)} %pad_clamp_fusion), kind=kCustom, calls=%fused_computation.1 | custom fusion | bytes 2098176 | tf_op jit(solution)/shard_map/jit(_take)/gather | solution.py:506
  235.0 0.0 copy-start.3
  235.0 0.0 copy-start.4
  235.0 0.0 copy-start.7
  235.0 0.0 copy-start.5
  235.0 0.0 copy-start.2
  235.0 0.7 gather.15
  235.8 0.0 copy-start.8
  235.8 0.1 reduce_sum.33
  235.9 0.1 copy.40
  236.0 0.0 copy-done.3
  236.0 0.1 copy.41
  236.2 0.0 copy-done.4
  236.2 0.1 fusion.5
  236.3 0.0 copy-done.7
  236.3 0.2 fusion.3
  236.5 0.0 copy-done.5
  236.5 0.1 copy.36
  236.6 4.1 %multiply_reduce_fusion = bf16[128,2048]{1,0:T(8,128)(2,1)S(1)} fusion(bf16[128,2,2048]{2,1,0:T(2,128)(2,1)S(1)} %gather.15, pred[128,2]{1,0:T(8,128)(4,1)S(1)} %copy.41, f32[128,2]{1,0:T(8,128)S(1)} %copy.36), kind=kLoop, calls=%fused_computation.4 | loop fusion | flops 1835008 | bytes 1574144 | tf_op jit(solution)/shard_map/reduce_sum | solution.py:522
  240.8 0.0 copy-done
  240.8 0.0 copy-done.2
  240.8 0.0 copy-start.1
  240.8 0.3 convolution_convert_fusion.1
  241.1 0.7 pad_convert_fusion.gate_ref
  241.8 0.7 dynamic_slice.3
  242.5 51.1 %delta_rule.1 = bf16[128,4096]{1,0:T(8,128)(2,1)} custom-call(bf16[4096,128]{1,0:T(8,128)(2,1)} %get-tuple-element.16.q_ref, bf16[4096,128]{1,0:T(8,128)(2,1)} %get-tuple-element.17.k_ref, bf16[4096,128]{1,0:T(8,128)(2,1)} %get-tuple-element.18.v_ref, bf16[4096,128]{1,0:T(8,128)(2,1)} %get-tuple-element.19.inv_ref, f32[32,8,128]{2,1,0:T(8,128)} %pad_convert_fusion.gate_ref, ...), custom_call_target="tpu_custom_call" | custom-call | tf_op jit(solution)/shard_map/delta_rule/pallas_call | solution.py:191
  293.6 2.3 copy.49
  (15 shorter events, 0.2 us)
Async XLA Ops:
  0.6 240.1 %copy-start = (bf16[2048,64]{0,1:T(8,128)(2,1)S(1)}, bf16[2048,64]{0,1:T(8,128)(2,1)}, u32[]{:S(2)}) copy-start(bf16[2048,64]{0,1:T(8,128)(2,1)} %param.22) | copy-start | bytes 786436
  121.6 3.6 %copy-start.6 = (bf16[16,32,2048]{2,1,0:T(8,128)(2,1)S(1)}, bf16[16,32,2048]{2,1,0:T(8,128)(2,1)}, u32[]{:S(2)}) copy-start(bf16[16,32,2048]{2,1,0:T(8,128)(2,1)} %get-tuple-element.11) | copy-start | bytes 6291460
  235.0 1.0 copy-start.3
  235.0 1.2 copy-start.4
  235.0 1.3 copy-start.7
  235.0 1.5 copy-start.5
  235.0 5.7 %copy-start.2 = (bf16[1,128,2048]{2,1,0:T(8,128)(2,1)S(1)}, bf16[1,128,2048]{2,1,0:T(8,128)(2,1)}, u32[]{:S(2)}) copy-start(bf16[1,128,2048]{2,1,0:T(8,128)(2,1)} %param.14) | copy-start | bytes 1572868
  235.8 6.0 %copy-start.8 = (f32[32]{0:T(128)S(1)}, f32[32]{0:T(128)}, u32[]{:S(2)}) copy-start(f32[32]{0:T(128)} %param.23) | copy-start | bytes 388
  240.8 52.8 %copy-start.1 = (bf16[128,2048]{1,0:T(8,128)(2,1)}, bf16[128,2048]{1,0:T(8,128)(2,1)S(1)}, u32[]{:S(2)}) copy-start(bf16[128,2048]{1,0:T(8,128)(2,1)S(1)} %multiply_reduce_fusion) | copy-start | bytes 1572868

commit v5 on v4

--- a/solution.py
+++ b/solution.py
@@ -315,14 +315,14 @@
         shard, full = pairs[i]
         return pltpu.make_async_copy(shard, slot(full, shard, seq_me), own_sem.at[i])
 
-    @pl.loop(1, exp_size)
-    def _(r):
-        block(r).start()
-
     @pl.loop(1, chips)
     def _(r):
         for i in range(3):
             spread(i, r).start()
+
+    @pl.loop(1, exp_size)
+    def _(r):
+        block(r).start()
 
     for i in range(3):
         hand_over(i).start()

time: 300 us -> 305 us (1.017)
  Pallas kernels: 262 us -> 269 us
    pallas_call x1, Pallas kernels: 51.1 us -> 57.9 us  [delta_rule(): pl.pallas_call(functools.partial(delta_kernel, block_size), grid=(seq_len...]
where the time goes in v5:
time: 305 us; the launch traced here: 303 us
  Pallas kernels  269 us (88%)
  local copies, waits for them, and re-layouts  15 us (5%)
  matrix products  10.2 us (3%)
  other arithmetic  8 us (3%)
    pallas_call x1, Pallas kernels, dispatch(): pl.pallas_call(dispatch_kernel, out_shape=(jax.ShapeDtypeStruct(rows.shap...  112 us
    pallas_call x1, Pallas kernels, give_back(): pl.pallas_call(return_kernel, out_shape=(jax.ShapeDtypeStruct(rows.shape,...  99.4 us
    pallas_call x1, Pallas kernels, delta_rule(): pl.pallas_call(functools.partial(delta_kernel, block_size), grid=(seq_len...  57.9 us

profile of v5, /device:TPU:1, one launch (start us, length us, event | category | flops | bytes accessed | tf_op | source)
XLA Modules:
  0.0 302.9 jit_solution(5868977012452499065)
XLA Ops:
  0.6 0.0 copy-start
  0.6 0.8 copy.37
  1.5 0.1 eq.74
  1.6 0.6 reduce-window.6
  2.2 0.2 slice_reduce_fusion
  2.4 0.1 reshape_squeeze.3
  2.6 0.1 fusion.8
  2.7 0.7 broadcast_multiply_fusion
  3.4 0.1 copy.42
  3.5 0.1 mul.65
  3.6 1.4 scatter_custom_fusion
  5.1 1.1 concatenate.3
  6.2 2.5 gather_fusion
  8.7 0.1 broadcast_in_dim.41
  8.7 1.6 broadcast_select_fusion.rows_ref
  10.4 111.5 %dispatch.1 = (bf16[16,32,2048]{2,1,0:T(8,128)(2,1)}, bf16[2048,512]{1,0:T(8,128)(2,1)}, bf16[2048,512]{1,0:T(8,128)(2,1)}, bf16[512,2048]{1,0:T(8,128)(2,1)}) custom-call(bf16[16,32,2048]{2,1,0:T(8,128)(2,1)} %broadcast_select_fusion.rows_ref, bf16[64,512]{1,0:T(8,128)(2,1)} %bitcast.70, bf16[64,512]{1,0:T(8,128)(2,1)} %bitcast.71, bf16[16,2048]{1,0:T(8,128)(2,1)} %bitcast.72), custom_call_target="tpu_custom_call" | custom-call | tf_op jit(solution)/shard_map/dispatch/pallas_call | solution.py:363
  121.9 0.0 copy-start.6
  121.9 3.6 %fusion.14 = f32[512,512]{1,0:T(8,128)S(1)} fusion(bf16[512,2048]{1,0:T(8,128)(2,1)} %bitcast.79, bf16[2048,512]{1,0:T(8,128)(2,1)} %get-tuple-element.12), kind=kOutput, calls=%fused_computation.49 | convolution fusion | flops 1073741824 | bytes 5242880 | tf_op jit(solution)/shard_map/dot_general | solution.py:495
  125.5 0.0 copy-done.6
  125.5 6.0 %convolution_convert_fusion = bf16[512,2048]{1,0:T(8,128)(2,1)} fusion(bf16[512,2048]{1,0:T(8,128)(2,1)} %get-tuple-element.14, bf16[512,2048]{1,0:T(8,128)(2,1)S(1)} %bitcast.80, bf16[2048,512]{1,0:T(8,128)(2,1)} %get-tuple-element.13, f32[512,512]{1,0:T(8,128)S(1)} %fusion.14), kind=kOutput, calls=%fused_computation.3 | convolution fusion | flops 2150105088 | bytes 9437184 | tf_op jit(solution)/shard_map/dot_general | solution.py:498
  131.6 99.4 %give_back.1 = (bf16[16,32,2048]{2,1,0:T(8,128)(2,1)}, bf16[4096,128]{1,0:T(8,128)(2,1)}, bf16[4096,128]{1,0:T(8,128)(2,1)}, bf16[4096,128]{1,0:T(8,128)(2,1)}, bf16[4096,128]{1,0:T(8,128)(2,1)}) custom-call(bf16[16,32,2048]{2,1,0:T(8,128)(2,1)} %bitcast.63, bf16[128,2048]{1,0:T(8,128)(2,1)} %bitcast.67, bf16[128,2048]{1,0:T(8,128)(2,1)} %bitcast.68, ...), custom_call_target="tpu_custom_call" | custom-call | tf_op jit(solution)/shard_map/give_back/pallas_call | solution.py:443
  231.0 4.2 %gather_fusion.1 = bf16[256,2048]{1,0:T(8,128)(2,1)S(1)} fusion(bf16[512,2048]{1,0:T(8,128)(2,1)} %bitcast.60, s32[1024]{0:T(1024)S(1)} %pad_clamp_fusion), kind=kCustom, calls=%fused_computation.1 | custom fusion | bytes 2098176 | tf_op jit(solution)/shard_map/jit(_take)/gather | solution.py:506
  235.3 0.0 copy-start.3
  235.3 0.0 copy-start.4
  235.3 0.0 copy-start.7
  235.3 0.0 copy-start.5
  235.3 0.0 copy-start.2
  235.3 0.7 gather.15
  236.0 0.0 copy-start.8
  236.1 0.1 reduce_sum.33
  236.2 0.1 copy.40
  236.3 0.0 copy-done.3
  236.3 0.1 copy.41
  236.4 0.0 copy-done.4
  236.4 0.1 fusion.5
  236.5 0.0 copy-done.7
  236.5 0.2 fusion.3
  236.8 0.0 copy-done.5
  236.8 0.1 copy.36
  236.9 4.1 %multiply_reduce_fusion = bf16[128,2048]{1,0:T(8,128)(2,1)S(1)} fusion(bf16[128,2,2048]{2,1,0:T(2,128)(2,1)S(1)} %gather.15, pred[128,2]{1,0:T(8,128)(4,1)S(1)} %copy.41, f32[128,2]{1,0:T(8,128)S(1)} %copy.36), kind=kLoop, calls=%fused_computation.4 | loop fusion | flops 1835008 | bytes 1574144 | tf_op jit(solution)/shard_map/reduce_sum | solution.py:522
  241.0 0.0 copy-done
  241.1 0.0 copy-done.2
  241.1 0.0 copy-start.1
  241.1 0.3 convolution_convert_fusion.1
  241.4 0.7 pad_convert_fusion.gate_ref
  242.1 0.7 dynamic_slice.3
  242.7 57.9 %delta_rule.1 = bf16[128,4096]{1,0:T(8,128)(2,1)} custom-call(bf16[4096,128]{1,0:T(8,128)(2,1)} %get-tuple-element.16.q_ref, bf16[4096,128]{1,0:T(8,128)(2,1)} %get-tuple-element.17.k_ref, bf16[4096,128]{1,0:T(8,128)(2,1)} %get-tuple-element.18.v_ref, bf16[4096,128]{1,0:T(8,128)(2,1)} %get-tuple-element.19.inv_ref, f32[32,8,128]{2,1,0:T(8,128)} %pad_convert_fusion.gate_ref, ...), custom_call_target="tpu_custom_call" | custom-call | tf_op jit(solution)/shard_map/delta_rule/pallas_call | solution.py:191
  300.6 2.3 copy.49
  (15 shorter events, 0.2 us)
Async XLA Ops:
  0.6 240.4 %copy-start = (bf16[2048,64]{0,1:T(8,128)(2,1)S(1)}, bf16[2048,64]{0,1:T(8,128)(2,1)}, u32[]{:S(2)}) copy-start(bf16[2048,64]{0,1:T(8,128)(2,1)} %param.22) | copy-start | bytes 786436
  121.9 3.6 %copy-start.6 = (bf16[16,32,2048]{2,1,0:T(8,128)(2,1)S(1)}, bf16[16,32,2048]{2,1,0:T(8,128)(2,1)}, u32[]{:S(2)}) copy-start(bf16[16,32,2048]{2,1,0:T(8,128)(2,1)} %get-tuple-element.11) | copy-start | bytes 6291460
  235.3 1.0 copy-start.3
  235.3 1.2 copy-start.4
  235.3 1.3 copy-start.7
  235.3 1.5 copy-start.5
  235.3 5.7 %copy-start.2 = (bf16[1,128,2048]{2,1,0:T(8,128)(2,1)S(1)}, bf16[1,128,2048]{2,1,0:T(8,128)(2,1)}, u32[]{:S(2)}) copy-start(bf16[1,128,2048]{2,1,0:T(8,128)(2,1)} %param.14) | copy-start | bytes 1572868
  236.0 6.0 %copy-start.8 = (f32[32]{0:T(128)S(1)}, f32[32]{0:T(128)}, u32[]{:S(2)}) copy-start(f32[32]{0:T(128)} %param.23) | copy-start | bytes 388
  241.1 59.5 %copy-start.1 = (bf16[128,2048]{1,0:T(8,128)(2,1)}, bf16[128,2048]{1,0:T(8,128)(2,1)S(1)}, u32[]{:S(2)}) copy-start(bf16[128,2048]{1,0:T(8,128)(2,1)S(1)} %multiply_reduce_fusion) | copy-start | bytes 1572868
